TPU v7x, 256 devices: a whole 4x4x8 slice. The times are simulated.
256 devices in a mesh: grp: 8 (over x_lo, y), tile: 32 (over z, x_hi, core).
Axes of the slice: x: 4 (x_hi: 2, x_lo: 2; x = x_hi * 2 + x_lo), y: 4, z: 8, core: 2. Of those that a mesh axis runs over, the one named last changes fastest.
Arguments:
- pool_input: float32 [64, 2048, 256], P('grp', 'tile'), may hold values from 0 to 20
- weight_first: bfloat16 [3, 3, 256, 512], replicated, may hold values from -0.125 to 0.125
- weight_second: bfloat16 [3, 3, 512, 512], replicated, may hold values from -0.09375 to 0.09375
- targets: float32 [2, 512, 512], replicated, may hold values from -0.3 to 0.3
Outputs:
- image_grad: float32 [64, 2048, 256], P('grp', 'tile')
All inputs are finite; a program needn't handle non-finite values.
Results may differ from a plain program's by a relative error of at most 0.0028.
Values may be sent and summed in bfloat16 or wider, within the bound.
A program may use at most 64 MiB of HBM per device.

v0:
```python
import jax
import jax.numpy as jnp
from jax import lax
from jax.sharding import Mesh
from jax.sharding import PartitionSpec as P

GRP_TILE = ("grp_0", "grp_1", "tile_0", "tile_1", "tile_2")
GRP = ("grp_0", "grp_1")
TILE = ("tile_0", "tile_1", "tile_2")


GELU_SCALE = 0.7978845608
GELU_CUBIC = 0.044715


def with_halo(array, sides, width):
    for axis, dim in sides:
        size, length = (lax.axis_size(axis), array.shape[dim])
        up = [(i, (i + 1) % size) for i in range(size - 1)]
        down = [(j, i) for i, j in up]
        last = lax.slice_in_dim(array, length - width, length, axis=dim)
        leading = lax.slice_in_dim(array, 0, width, axis=dim)
        before = lax.ppermute(last, axis, up)
        after = lax.ppermute(leading, axis, down)
        array = jnp.concatenate([before, array, after], axis=dim)
    return array


def by_axis(array, axes):
    for axis in axes:
        array = lax.psum(array, axis)
    return array


def cut_along(array, dim, size):
    shape = array.shape
    tiles = array.reshape(*shape[:dim], size, shape[dim] // size, *shape[dim + 1 :])
    return jnp.moveaxis(tiles, dim, 0)


def summed_on_arrival(array, axis, dim):
    size = lax.axis_size(axis)
    tiles = lax.all_to_all(cut_along(array, dim, size), axis, 0, 0, tiled=True)
    return jnp.sum(tiles.astype(jnp.float32), axis=0)


def copy_for_each(array, axis):
    copies = jnp.broadcast_to(array, (lax.axis_size(axis), *array.shape))
    return lax.all_to_all(copies, axis, split_axis=0, concat_axis=0, tiled=True)


def over_copies(array, axis):
    everything = copy_for_each(array, axis)
    return jnp.sum(everything, axis=0)


def gelu_value(values):
    return 0.5 * values * (1.0 + jnp.tanh(GELU_SCALE * (values + GELU_CUBIC * values**3)))


def gelu_slope(values):
    hyper = jnp.tanh(GELU_SCALE * (values + GELU_CUBIC * values**3))
    return 0.5 * (1.0 + hyper) + 0.5 * values * (1.0 - hyper * hyper) * GELU_SCALE * (
        1.0 + 3.0 * GELU_CUBIC * values * values
    )


def conv_fwd(padded, weight, height, breadth):
    summed = None
    for row_shift in range(3):
        for col_shift in range(3):
            window = padded[
                row_shift : row_shift + height, col_shift : col_shift + breadth, :
            ].reshape(height * breadth, -1)
            product = jnp.dot(
                window, weight[row_shift, col_shift], preferred_element_type=jnp.float32
            )
            summed = product if summed is None else summed + product
    return summed.reshape(height, breadth, -1)


def conv_back(padded, weight, height, breadth):
    summed = None
    for row_shift in range(3):
        for col_shift in range(3):
            window = padded[
                2 - row_shift : 2 - row_shift + height, 2 - col_shift : 2 - col_shift + breadth, :
            ].reshape(height * breadth, -1)
            product = lax.dot_general(
                window,
                weight[row_shift, col_shift],
                (((1,), (1,)), ((), ())),
                preferred_element_type=jnp.float32,
            )
            summed = product if summed is None else summed + product
    return summed.reshape(height, breadth, -1)


def inner_dot(left, right):
    return lax.dot_general(
        left,
        right,
        (((0,), (0,)), ((), ())),
        precision=lax.Precision.HIGHEST,
        preferred_element_type=jnp.float32,
    )


def local(pool_input, weight_first, weight_second, targets):
    tile_rows = pool_input.shape[0]
    tile_cols = pool_input.shape[1]
    width_out = weight_first.shape[3]
    pool_bf = pool_input.astype(jnp.bfloat16)
    reach = 1
    padded_pool = with_halo(pool_bf, ((GRP, 0), (TILE, 1)), reach)
    pre_first = conv_fwd(padded_pool, weight_first, tile_rows, tile_cols)
    act_first = gelu_value(pre_first)
    padded_first = with_halo(act_first.astype(jnp.bfloat16), ((GRP, 0), (TILE, 1)), 1)
    pre_second = conv_fwd(padded_first, weight_second, tile_rows, tile_cols)
    act_second = gelu_value(pre_second)
    flat_first = act_first.reshape(-1, width_out)
    flat_second = act_second.reshape(-1, width_out)
    positions = tile_rows * tile_cols * lax.axis_size(GRP) * lax.axis_size(TILE)
    column_sums = (
        by_axis(jnp.sum(flat_first, axis=0), GRP_TILE),
        by_axis(jnp.sum(flat_second, axis=0), GRP_TILE),
    )
    mean_first = column_sums[0] / positions
    mean_second = column_sums[1] / positions
    centred_first = flat_first - mean_first
    centred_second = flat_second - mean_second
    left_first, left_second = (centred_first, centred_second)
    share_rows = width_out // lax.axis_size(TILE)
    gram_share = summed_on_arrival(
        jnp.concatenate(
            [inner_dot(left_first, left_first), inner_dot(left_second, left_second)], axis=1
        ).astype(jnp.bfloat16),
        TILE,
        0,
    )
    gram_share = over_copies(gram_share, GRP)
    offset = lax.axis_index(TILE) * share_rows
    gram_first = gram_share[:, :width_out] / positions
    gram_second = gram_share[:, width_out:] / positions
    miss_first = gram_first - lax.dynamic_slice_in_dim(targets[0], offset, share_rows, 0)
    miss_second = gram_second - lax.dynamic_slice_in_dim(targets[1], offset, share_rows, 0)
    diff_share = jnp.concatenate([miss_first, miss_second], axis=1)
    mismatch = lax.all_gather(diff_share, TILE, axis=0, tiled=True)
    miss_first = mismatch[:, :width_out]
    miss_second = mismatch[:, width_out:]
    symmetric_first = (miss_first + miss_first.T) * 0.5
    symmetric_second = (miss_second + miss_second.T) * 0.5
    push_first = jnp.dot(
        centred_first,
        symmetric_first,
        precision=lax.Precision.HIGHEST,
        preferred_element_type=jnp.float32,
    ).reshape(tile_rows, tile_cols, width_out)
    push_second = jnp.dot(
        centred_second,
        symmetric_second,
        precision=lax.Precision.HIGHEST,
        preferred_element_type=jnp.float32,
    ).reshape(tile_rows, tile_cols, width_out)
    grad_second = (push_second * gelu_slope(pre_second)).astype(jnp.bfloat16)
    padded_second = with_halo(grad_second, ((GRP, 0), (TILE, 1)), 1)
    flow_first = push_first + conv_back(padded_second, weight_second, tile_rows, tile_cols)
    grad_first = (flow_first * gelu_slope(pre_first)).astype(jnp.bfloat16)
    padded_grad = with_halo(grad_first, ((GRP, 0), (TILE, 1)), 1)
    return conv_back(padded_grad, weight_first, tile_rows, tile_cols)


def solution(mesh):
    finer = Mesh(
        mesh.devices.reshape(2, 4, 8, 2, 2), ("grp_0", "grp_1", "tile_0", "tile_1", "tile_2")
    )
    return jax.shard_map(
        local,
        mesh=finer,
        in_specs=(P(GRP, TILE, None), P(), P(), P()),
        out_specs=P(GRP, TILE, None),
        check_vma=False,
    )
```

profile of v0, /device:TPU:152, one launch (start us, length us, event | category | flops | bytes accessed | tf_op | source)
XLA Modules:
  0.0 301.7 jit_solution(18018562271018855900)
XLA Ops:
  7.6 3.1 %collective-permute-start = (bf16[1,64,256]{2,1,0:T(8,128)(2,1)S(1)}, bf16[1,64,256]{2,1,0:T(8,128)(2,1)S(1)}, u32[]{:S(2)}, u32[]{:S(2)}) collective-permute-start(bf16[1,64,256]{2,1,0:T(8,128)(2,1)S(1)} %get-tuple-element.73), channel_id=1, source_target_pairs={{0,32},{32,64},{64,96},{96,128},{128,160},{160,192},{192,224},{1,3... | collective-permute-start | bytes 98312 | tf_op jit(solution)/shard_map/ppermute | solution.py:23
  10.7 2.8 collective-permute-start.1
  13.5 5.1 %collective-permute-done.1 = bf16[1,64,256]{2,1,0:T(8,128)(2,1)S(1)} collective-permute-done((bf16[1,64,256]{2,1,0:T(8,128)(2,1)S(1)}, bf16[1,64,256]{2,1,0:T(8,128)(2,1)S(1)}, u32[]{:S(2)}, u32[]{:S(2)}) %collective-permute-start.1) | collective-permute-done | bytes 32800 | tf_op jit(solution)/shard_map/ppermute | solution.py:24
  20.6 7.3 %collective-permute-start.3 = (bf16[10,1,256]{2,1,0:T(2,128)(2,1)S(1)}, bf16[10,1,256]{2,1,0:T(2,128)(2,1)S(1)}, u32[]{:S(2)}, u32[]{:S(2)}) collective-permute-start(bf16[10,1,256]{2,1,0:T(2,128)(2,1)S(1)} %get-tuple-element.70), channel_id=1, source_target_pairs={{1,0},{2,1},{3,2},{4,3},{5,4},{6,5},{7,6},{8,7},{9,8},{10,9},{11,1... | collective-permute-start | bytes 15368 | tf_op jit(solution)/shard_map/ppermute | solution.py:24
  33.8 2.1 collective-permute-start.4
  35.9 3.9 %collective-permute-start.5 = (bf16[1,64,512]{2,1,0:T(8,128)(2,1)S(1)}, bf16[1,64,512]{2,1,0:T(8,128)(2,1)S(1)}, u32[]{:S(2)}, u32[]{:S(2)}) collective-permute-start(bf16[1,64,512]{2,1,0:T(8,128)(2,1)S(1)} %get-tuple-element.60), channel_id=1, source_target_pairs={{32,0},{64,32},{96,64},{128,96},{160,128},{192,160},{224,192},{33,... | collective-permute-start | bytes 196616 | tf_op jit(solution)/shard_map/ppermute | solution.py:24
  40.1 4.0 %collective-permute-done.5 = bf16[1,64,512]{2,1,0:T(8,128)(2,1)S(1)} collective-permute-done((bf16[1,64,512]{2,1,0:T(8,128)(2,1)S(1)}, bf16[1,64,512]{2,1,0:T(8,128)(2,1)S(1)}, u32[]{:S(2)}, u32[]{:S(2)}) %collective-permute-start.5) | collective-permute-done | bytes 65568 | tf_op jit(solution)/shard_map/ppermute | solution.py:24
  46.1 7.3 %collective-permute-start.7 = (bf16[10,1,512]{2,1,0:T(2,128)(2,1)S(1)}, bf16[10,1,512]{2,1,0:T(2,128)(2,1)S(1)}, u32[]{:S(2)}, u32[]{:S(2)}) collective-permute-start(bf16[10,1,512]{2,1,0:T(2,128)(2,1)S(1)} %get-tuple-element.48), channel_id=1, source_target_pairs={{1,0},{2,1},{3,2},{4,3},{5,4},{6,5},{7,6},{8,7},{9,8},{10,9},{11,1... | collective-permute-start | bytes 30728 | tf_op jit(solution)/shard_map/ppermute | solution.py:24
  59.5 4.9 %all-reduce.4 = (f32[512]{0:T(512)S(1)}, f32[512]{0:T(512)S(1)}) all-reduce(f32[512]{0:T(512)S(1)} %get-tuple-element.77, f32[512]{0:T(512)S(1)} %get-tuple-element.79), channel_id=1, replica_groups=mesh['grp_0'=2,'grp_1'=4,'tile_0'=8,'tile_1'=2,'tile_2'=2] {'grp_0'}, use_global_device_ids=true, to_apply=%region_1.0 | all-reduce | flops 1024 | bytes 8192 | tf_op jit(solution)/shard_map/psum | solution.py:31
  64.4 7.4 %all-reduce.1 = (f32[512]{0:T(512)S(1)}, f32[512]{0:T(512)S(1)}) all-reduce(f32[512]{0:T(512)S(1)} %get-tuple-element.13, f32[512]{0:T(512)S(1)} %get-tuple-element.14), channel_id=1, replica_groups=mesh['grp_0'=2,'grp_1'=4,'tile_0'=8,'tile_1'=2,'tile_2'=2] {'grp_1'}, use_global_device_ids=true, to_apply=%region_2.0 | all-reduce | flops 1024 | bytes 8192 | tf_op jit(solution)/shard_map/psum | solution.py:31
  71.9 14.1 %all-reduce = (f32[512]{0:T(512)S(1)}, f32[512]{0:T(512)S(1)}) all-reduce(f32[512]{0:T(512)S(1)} %get-tuple-element.7, f32[512]{0:T(512)S(1)} %get-tuple-element.8), channel_id=1, replica_groups=mesh['grp_0'=2,'grp_1'=4,'tile_0'=8,'tile_1'=2,'tile_2'=2] {'tile_0'}, use_global_device_ids=true, to_apply=%region_3.0 | all-reduce | flops 1024 | bytes 8192 | tf_op jit(solution)/shard_map/psum | solution.py:31
  86.0 6.4 %all-reduce.3 = (f32[512]{0:T(512)S(1)}, f32[512]{0:T(512)S(1)}) all-reduce(f32[512]{0:T(512)S(1)} %get-tuple-element.5, f32[512]{0:T(512)S(1)} %get-tuple-element.6), channel_id=1, replica_groups=mesh['grp_0'=2,'grp_1'=4,'tile_0'=8,'tile_1'=2,'tile_2'=2] {'tile_1'}, use_global_device_ids=true, to_apply=%region_4.0 | all-reduce | flops 1024 | bytes 8192 | tf_op jit(solution)/shard_map/psum | solution.py:31
  92.4 2.6 all-reduce.2
  99.7 33.4 %all_to_all.10 = bf16[32,16,1024]{2,1,0:T(8,128)(2,1)S(1)} all-to-all(bf16[32,16,1024]{2,1,0:T(8,128)(2,1)S(1)} %pad_maximum_fusion), channel_id=1, replica_groups=mesh['grp_0'=2,'grp_1'=4,'tile_0'=8,'tile_1'=2,'tile_2'=2] {'tile_0','ti..., dimensions={0} | all-to-all | bytes 2097152 | tf_op jit(solution)/shard_map/all_to_all | solution.py:43
  134.1 6.9 %all-to-all-start.1 = ((f32[8,16,1024]{2,1,0:T(8,128)}), f32[8,16,1024]{2,1,0:T(8,128)S(1)}, u32[]{:S(2)}, u32[]{:S(2)}) async-start(f32[8,16,1024]{2,1,0:T(8,128)} %broadcast_in_dim.2), calls=%async_computation.1 | async-start | bytes 1048576 | tf_op jit(solution)/shard_map/all_to_all | solution.py:49
  141.0 3.1 %fusion.133 = (f32[1,512,512]{2,1,0:T(8,128)}, f32[1,512,512]{2,1,0:T(8,128)}) fusion(f32[2,512,512]{2,1,0:T(8,128)} %param.7), kind=kLoop, calls=%fused_computation.207 | loop fusion | bytes 4194304 | tf_op jit(solution)/shard_map/slice | solution.py:145
  144.1 5.5 %all-to-all-done.1 = f32[8,16,1024]{2,1,0:T(8,128)S(1)} async-done(((f32[8,16,1024]{2,1,0:T(8,128)}), f32[8,16,1024]{2,1,0:T(8,128)S(1)}, u32[]{:S(2)}, u32[]{:S(2)}) %all-to-all-start.1) | async-done | bytes 524320 | tf_op jit(solution)/shard_map/all_to_all | solution.py:49
  151.0 76.5 %all-gather.2.cloned.1.call-done = f32[512,1024]{1,0:T(8,128)} async-done(((f32[16,1024]{1,0:T(8,128)}), f32[512,1024]{1,0:T(8,128)}) %all-gather.2.cloned.1.call-update) | async-done | bytes 2097168 | tf_op jit(solution)/shard_map/all_gather | solution.py:148
  227.5 2.7 fusion.132
  231.5 4.6 %fusion.3 = bf16[8,64,512]{2,1,0:T(8,128)(2,1)S(1)} fusion(f32[8,64,512]{2,1,0:T(8,128)} %bitcast.211, f32[8,64,512]{2,1,0:T(8,128)} %bitcast.244, f32[512,512]{0,1:T(8,128)} %copy.20, f32[512,1024]{1,0:T(8,128)} %all-gather.2.cloned.1.call-done), kind=kOutput, calls=%fused_computation.32 | convolution fusion | flops 1616117760 | bytes 4718592 | tf_op jit(solution)/shard_map/dot_general | solution.py:159
  236.2 2.4 collective-permute-start.8
  238.6 3.4 %collective-permute-start.9 = (bf16[1,64,512]{2,1,0:T(8,128)(2,1)S(1)}, bf16[1,64,512]{2,1,0:T(8,128)(2,1)S(1)}, u32[]{:S(2)}, u32[]{:S(2)}) collective-permute-start(bf16[1,64,512]{2,1,0:T(8,128)(2,1)S(1)} %get-tuple-element.56), channel_id=1, source_target_pairs={{32,0},{64,32},{96,64},{128,96},{160,128},{192,160},{224,192},{33,... | collective-permute-start | bytes 196616 | tf_op jit(solution)/shard_map/ppermute | solution.py:24
  242.0 2.5 copy.19
  244.6 3.6 %fusion.36 = f32[8,64,512]{2,1,0:T(8,128)S(1)} fusion(f32[8,64,512]{2,1,0:T(8,128)S(1)} %bitcast.204, f32[512,512]{0,1:T(8,128)} %copy.19, f32[512,1024]{1,0:T(8,128)} %all-gather.2.cloned.1.call-done), kind=kOutput, calls=%fused_computation.75 | convolution fusion | flops 1611137024 | bytes 4194304 | tf_op jit(solution)/shard_map/dot_general | solution.py:153
  248.2 4.1 %collective-permute-start.10 = (bf16[10,1,512]{2,1,0:T(2,128)(2,1)S(1)}, bf16[10,1,512]{2,1,0:T(2,128)(2,1)S(1)}, u32[]{:S(2)}, u32[]{:S(2)}) collective-permute-start(bf16[10,1,512]{2,1,0:T(2,128)(2,1)S(1)} %get-tuple-element.43), channel_id=1, source_target_pairs={{1,0},{2,1},{3,2},{4,3},{5,4},{6,5},{7,6},{8,7},{9,8},{10,9},{11,1... | collective-permute-start | bytes 30728 | tf_op jit(solution)/shard_map/ppermute | solution.py:24
  252.3 2.1 collective-permute-start.11
  256.2 4.9 %collective-permute-done.11 = bf16[10,1,512]{2,1,0:T(2,128)(2,1)S(1)} collective-permute-done((bf16[10,1,512]{2,1,0:T(2,128)(2,1)S(1)}, bf16[10,1,512]{2,1,0:T(2,128)(2,1)S(1)}, u32[]{:S(2)}, u32[]{:S(2)}) %collective-permute-start.11) | collective-permute-done | bytes 10272 | tf_op jit(solution)/shard_map/ppermute | solution.py:23
  266.3 5.1 %collective-permute-start.12 = (bf16[1,64,512]{2,1,0:T(8,128)(2,1)S(1)}, bf16[1,64,512]{2,1,0:T(8,128)(2,1)S(1)}, u32[]{:S(2)}, u32[]{:S(2)}) collective-permute-start(bf16[1,64,512]{2,1,0:T(8,128)(2,1)S(1)} %get-tuple-element.51), channel_id=1, source_target_pairs={{0,32},{32,64},{64,96},{96,128},{128,160},{160,192},{192,224},{1,3... | collective-permute-start | bytes 196616 | tf_op jit(solution)/shard_map/ppermute | solution.py:23
  273.4 6.3 %collective-permute-done.13 = bf16[1,64,512]{2,1,0:T(8,128)(2,1)S(1)} collective-permute-done((bf16[1,64,512]{2,1,0:T(8,128)(2,1)S(1)}, bf16[1,64,512]{2,1,0:T(8,128)(2,1)S(1)}, u32[]{:S(2)}, u32[]{:S(2)}) %collective-permute-start.13) | collective-permute-done | bytes 65568 | tf_op jit(solution)/shard_map/ppermute | solution.py:24
  279.8 2.2 collective-permute-start.14
  282.0 2.1 collective-permute-start.15
  284.6 6.1 %collective-permute-done.15 = bf16[10,1,512]{2,1,0:T(2,128)(2,1)S(1)} collective-permute-done((bf16[10,1,512]{2,1,0:T(2,128)(2,1)S(1)}, bf16[10,1,512]{2,1,0:T(2,128)(2,1)S(1)}, u32[]{:S(2)}, u32[]{:S(2)}) %collective-permute-start.15) | collective-permute-done | bytes 10272 | tf_op jit(solution)/shard_map/ppermute | solution.py:23
  (109 shorter events, 38.8 us)
Async XLA Ops:
  7.6 5.9 %collective-permute-start = (bf16[1,64,256]{2,1,0:T(8,128)(2,1)S(1)}, bf16[1,64,256]{2,1,0:T(8,128)(2,1)S(1)}, u32[]{:S(2)}, u32[]{:S(2)}) collective-permute-start(bf16[1,64,256]{2,1,0:T(8,128)(2,1)S(1)} %get-tuple-element.73), channel_id=1, source_target_pairs={{0,32},{32,64},{64,96},{96,128},{128,160},{160,192},{192,224},{1,3... | collective-permute-start | bytes 98312 | tf_op jit(solution)/shard_map/ppermute | solution.py:23
  10.7 7.9 %collective-permute-start.1 = (bf16[1,64,256]{2,1,0:T(8,128)(2,1)S(1)}, bf16[1,64,256]{2,1,0:T(8,128)(2,1)S(1)}, u32[]{:S(2)}, u32[]{:S(2)}) collective-permute-start(bf16[1,64,256]{2,1,0:T(8,128)(2,1)S(1)} %get-tuple-element.74), channel_id=1, source_target_pairs={{32,0},{64,32},{96,64},{128,96},{160,128},{192,160},{224,192},{33,... | collective-permute-start | bytes 98312 | tf_op jit(solution)/shard_map/ppermute | solution.py:24
  18.6 10.5 %collective-permute-start.2 = (bf16[10,1,256]{2,1,0:T(2,128)(2,1)S(1)}, bf16[10,1,256]{2,1,0:T(2,128)(2,1)S(1)}, u32[]{:S(2)}, u32[]{:S(2)}) collective-permute-start(bf16[10,1,256]{2,1,0:T(2,128)(2,1)S(1)} %get-tuple-element.69), channel_id=1, source_target_pairs={{0,1},{1,2},{2,3},{3,4},{4,5},{5,6},{6,7},{7,8},{8,9},{9,10},{10,1... | collective-permute-start | bytes 15368 | tf_op jit(solution)/shard_map/ppermute | solution.py:23
  20.6 8.6 %collective-permute-start.3 = (bf16[10,1,256]{2,1,0:T(2,128)(2,1)S(1)}, bf16[10,1,256]{2,1,0:T(2,128)(2,1)S(1)}, u32[]{:S(2)}, u32[]{:S(2)}) collective-permute-start(bf16[10,1,256]{2,1,0:T(2,128)(2,1)S(1)} %get-tuple-element.70), channel_id=1, source_target_pairs={{1,0},{2,1},{3,2},{4,3},{5,4},{6,5},{7,6},{8,7},{9,8},{10,9},{11,1... | collective-permute-start | bytes 15368 | tf_op jit(solution)/shard_map/ppermute | solution.py:24
  29.1 1.7 copy-start
  32.6 20.9 %slice-start = ((s8[4718592]{0:T(1024)(128)(4,1)}), s8[4194304]{0:T(1024)(128)(4,1)S(1)}, s32[]{:S(2)}) async-start(s8[4718592]{0:T(1024)(128)(4,1)} %bitcast.205), calls=%async_computation.3 | async-start | bytes 8388608
  32.9 20.6 %slice-start.1 = ((s8[4718592]{0:T(1024)(128)(4,1)}), s8[524288]{0:T(1024)(128)(4,1)S(1)}, s32[]{:S(2)}) async-start(s8[4718592]{0:T(1024)(128)(4,1)} %bitcast.205), calls=%async_computation.4 | async-start | bytes 1048576
  33.8 6.3 %collective-permute-start.4 = (bf16[1,64,512]{2,1,0:T(8,128)(2,1)S(1)}, bf16[1,64,512]{2,1,0:T(8,128)(2,1)S(1)}, u32[]{:S(2)}, u32[]{:S(2)}) collective-permute-start(bf16[1,64,512]{2,1,0:T(8,128)(2,1)S(1)} %get-tuple-element.59), channel_id=1, source_target_pairs={{0,32},{32,64},{64,96},{96,128},{128,160},{160,192},{192,224},{1,3... | collective-permute-start | bytes 196616 | tf_op jit(solution)/shard_map/ppermute | solution.py:23
  35.9 8.3 %collective-permute-start.5 = (bf16[1,64,512]{2,1,0:T(8,128)(2,1)S(1)}, bf16[1,64,512]{2,1,0:T(8,128)(2,1)S(1)}, u32[]{:S(2)}, u32[]{:S(2)}) collective-permute-start(bf16[1,64,512]{2,1,0:T(8,128)(2,1)S(1)} %get-tuple-element.60), channel_id=1, source_target_pairs={{32,0},{64,32},{96,64},{128,96},{160,128},{192,160},{224,192},{33,... | collective-permute-start | bytes 196616 | tf_op jit(solution)/shard_map/ppermute | solution.py:24
  44.2 9.7 %collective-permute-start.6 = (bf16[10,1,512]{2,1,0:T(2,128)(2,1)S(1)}, bf16[10,1,512]{2,1,0:T(2,128)(2,1)S(1)}, u32[]{:S(2)}, u32[]{:S(2)}) collective-permute-start(bf16[10,1,512]{2,1,0:T(2,128)(2,1)S(1)} %get-tuple-element.47), channel_id=1, source_target_pairs={{0,1},{1,2},{2,3},{3,4},{4,5},{5,6},{6,7},{7,8},{8,9},{9,10},{10,1... | collective-permute-start | bytes 30728 | tf_op jit(solution)/shard_map/ppermute | solution.py:23
  46.1 8.7 %collective-permute-start.7 = (bf16[10,1,512]{2,1,0:T(2,128)(2,1)S(1)}, bf16[10,1,512]{2,1,0:T(2,128)(2,1)S(1)}, u32[]{:S(2)}, u32[]{:S(2)}) collective-permute-start(bf16[10,1,512]{2,1,0:T(2,128)(2,1)S(1)} %get-tuple-element.48), channel_id=1, source_target_pairs={{1,0},{2,1},{3,2},{4,3},{5,4},{6,5},{7,6},{8,7},{9,8},{10,9},{11,1... | collective-permute-start | bytes 30728 | tf_op jit(solution)/shard_map/ppermute | solution.py:24
  59.5 35.9 %copy-start.3 = (f32[512,512]{1,0:T(8,128)}, f32[512,512]{1,0:T(8,128)S(1)}, u32[]{:S(2)}) copy-start(f32[512,512]{1,0:T(8,128)S(1)} %get-tuple-element.80) | copy-start | bytes 3145732
  95.4 2.2 copy-start.2
  134.1 15.5 %all-to-all-start.1 = ((f32[8,16,1024]{2,1,0:T(8,128)}), f32[8,16,1024]{2,1,0:T(8,128)S(1)}, u32[]{:S(2)}, u32[]{:S(2)}) async-start(f32[8,16,1024]{2,1,0:T(8,128)} %broadcast_in_dim.2), calls=%async_computation.1 | async-start | bytes 1048576 | tf_op jit(solution)/shard_map/all_to_all | solution.py:49
  141.0 86.5 %all-gather.2.cloned.1.call-start = ((), (), s32[]{:S(2)}) async-start(), calls=%async_computation.2 | async-start | bytes 2162688 | tf_op jit(solution)/shard_map/all_gather | solution.py:148
  236.2 12.0 %collective-permute-start.8 = (bf16[1,64,512]{2,1,0:T(8,128)(2,1)S(1)}, bf16[1,64,512]{2,1,0:T(8,128)(2,1)S(1)}, u32[]{:S(2)}, u32[]{:S(2)}) collective-permute-start(bf16[1,64,512]{2,1,0:T(8,128)(2,1)S(1)} %get-tuple-element.55), channel_id=1, source_target_pairs={{0,32},{32,64},{64,96},{96,128},{128,160},{160,192},{192,224},{1,3... | collective-permute-start | bytes 196616 | tf_op jit(solution)/shard_map/ppermute | solution.py:23
  238.6 9.6 %collective-permute-start.9 = (bf16[1,64,512]{2,1,0:T(8,128)(2,1)S(1)}, bf16[1,64,512]{2,1,0:T(8,128)(2,1)S(1)}, u32[]{:S(2)}, u32[]{:S(2)}) collective-permute-start(bf16[1,64,512]{2,1,0:T(8,128)(2,1)S(1)} %get-tuple-element.56), channel_id=1, source_target_pairs={{32,0},{64,32},{96,64},{128,96},{160,128},{192,160},{224,192},{33,... | collective-permute-start | bytes 196616 | tf_op jit(solution)/shard_map/ppermute | solution.py:24
  244.6 17.2 %slice-start.2 = ((s8[4718592]{0:T(1024)(128)(4,1)}), s8[4194304]{0:T(1024)(128)(4,1)S(1)}, s32[]{:S(2)}) async-start(s8[4718592]{0:T(1024)(128)(4,1)} %bitcast.207), calls=%async_computation.5 | async-start | bytes 8388608
  248.2 7.9 %collective-permute-start.10 = (bf16[10,1,512]{2,1,0:T(2,128)(2,1)S(1)}, bf16[10,1,512]{2,1,0:T(2,128)(2,1)S(1)}, u32[]{:S(2)}, u32[]{:S(2)}) collective-permute-start(bf16[10,1,512]{2,1,0:T(2,128)(2,1)S(1)} %get-tuple-element.43), channel_id=1, source_target_pairs={{1,0},{2,1},{3,2},{4,3},{5,4},{6,5},{7,6},{8,7},{9,8},{10,9},{11,1... | collective-permute-start | bytes 30728 | tf_op jit(solution)/shard_map/ppermute | solution.py:24
  252.3 8.7 %collective-permute-start.11 = (bf16[10,1,512]{2,1,0:T(2,128)(2,1)S(1)}, bf16[10,1,512]{2,1,0:T(2,128)(2,1)S(1)}, u32[]{:S(2)}, u32[]{:S(2)}) collective-permute-start(bf16[10,1,512]{2,1,0:T(2,128)(2,1)S(1)} %get-tuple-element.44), channel_id=1, source_target_pairs={{0,1},{1,2},{2,3},{3,4},{4,5},{5,6},{6,7},{7,8},{8,9},{9,10},{10,1... | collective-permute-start | bytes 30728 | tf_op jit(solution)/shard_map/ppermute | solution.py:23
  254.6 7.2 %slice-start.3 = ((s8[4718592]{0:T(1024)(128)(4,1)}), s8[524288]{0:T(1024)(128)(4,1)S(1)}, s32[]{:S(2)}) async-start(s8[4718592]{0:T(1024)(128)(4,1)} %bitcast.207), calls=%async_computation.6 | async-start | bytes 1048576
  265.6 18.6 %copy-start.1 = (bf16[3,3,256,512]{3,2,1,0:T(8,128)(2,1)S(1)}, bf16[3,3,256,512]{3,2,1,0:T(8,128)(2,1)}, u32[]{:S(2)}) copy-start(bf16[3,3,256,512]{3,2,1,0:T(8,128)(2,1)} %param.5) | copy-start | bytes 7077892
  266.3 7.1 %collective-permute-start.12 = (bf16[1,64,512]{2,1,0:T(8,128)(2,1)S(1)}, bf16[1,64,512]{2,1,0:T(8,128)(2,1)S(1)}, u32[]{:S(2)}, u32[]{:S(2)}) collective-permute-start(bf16[1,64,512]{2,1,0:T(8,128)(2,1)S(1)} %get-tuple-element.51), channel_id=1, source_target_pairs={{0,32},{32,64},{64,96},{96,128},{128,160},{160,192},{192,224},{1,3... | collective-permute-start | bytes 196616 | tf_op jit(solution)/shard_map/ppermute | solution.py:23
  271.5 8.3 %collective-permute-start.13 = (bf16[1,64,512]{2,1,0:T(8,128)(2,1)S(1)}, bf16[1,64,512]{2,1,0:T(8,128)(2,1)S(1)}, u32[]{:S(2)}, u32[]{:S(2)}) collective-permute-start(bf16[1,64,512]{2,1,0:T(8,128)(2,1)S(1)} %get-tuple-element.52), channel_id=1, source_target_pairs={{32,0},{64,32},{96,64},{128,96},{160,128},{192,160},{224,192},{33,... | collective-permute-start | bytes 196616 | tf_op jit(solution)/shard_map/ppermute | solution.py:24
  279.8 4.8 %collective-permute-start.14 = (bf16[10,1,512]{2,1,0:T(2,128)(2,1)S(1)}, bf16[10,1,512]{2,1,0:T(2,128)(2,1)S(1)}, u32[]{:S(2)}, u32[]{:S(2)}) collective-permute-start(bf16[10,1,512]{2,1,0:T(2,128)(2,1)S(1)} %get-tuple-element.39), channel_id=1, source_target_pairs={{1,0},{2,1},{3,2},{4,3},{5,4},{6,5},{7,6},{8,7},{9,8},{10,9},{11,1... | collective-permute-start | bytes 30728 | tf_op jit(solution)/shard_map/ppermute | solution.py:24
  282.0 8.7 %collective-permute-start.15 = (bf16[10,1,512]{2,1,0:T(2,128)(2,1)S(1)}, bf16[10,1,512]{2,1,0:T(2,128)(2,1)S(1)}, u32[]{:S(2)}, u32[]{:S(2)}) collective-permute-start(bf16[10,1,512]{2,1,0:T(2,128)(2,1)S(1)} %get-tuple-element.40), channel_id=1, source_target_pairs={{0,1},{1,2},{2,3},{3,4},{4,5},{5,6},{6,7},{7,8},{8,9},{9,10},{10,1... | collective-permute-start | bytes 30728 | tf_op jit(solution)/shard_map/ppermute | solution.py:23
Sparse Core Ops, SparseCore 0:
  151.1 76.2 all-gather.1
where the time goes:
time: 303 us; the launch traced here: 302 us
  waiting for transfers between devices  110 us (36%)
  blocking collectives  69 us (23%)
  starting transfers between devices  60.6 us (20%)
  matrix products  29.2 us (10%)
  between operations  14.2 us (5%)
  local copies, waits for them, and re-layouts  13.3 us (4%)
  other arithmetic  5.86 us (2%)
    all_gather x1, waiting for transfers between devices, local(): mismatch = lax.all_gather(diff_share, TILE, axis=0, tiled=True)  76.5 us
    psum x5, blocking collectives, by_axis(): array = lax.psum(array, axis)  35.6 us
    all_to_all x1, blocking collectives, summed_on_arrival(): tiles = lax.all_to_all(cut_along(array, dim, size), axis, 0, 0, tiled=True)  33.4 us
    ppermute x8, starting transfers between devices, with_halo(): after = lax.ppermute(leading, axis, down)  32.9 us
    ppermute x8, starting transfers between devices, with_halo(): before = lax.ppermute(last, axis, up)  20.8 us
    ppermute x8, waiting for transfers between devices, with_halo(): after = lax.ppermute(leading, axis, down)  16.4 us
    ppermute x8, waiting for transfers between devices, with_halo(): before = lax.ppermute(last, axis, up)  11.3 us
    dot_general x18, matrix products, conv_back(): lax.dot_general(window, weight[row_shift, col_shift], (((1,), (1,)), ((),...  9.12 us
  transfers between devices with their start and end apart: 18, of which 10 were waited for; matrix products, arithmetic and copies ran while one was open for 4% of the time, Pallas kernels for 0%

commit v1 on v0

v1 whole, which is shorter than its diff:
```python
import functools

import jax
import jax.numpy as jnp
from jax import lax
from jax.experimental import pallas as pl
from jax.experimental.pallas import tpu as pltpu
from jax.sharding import PartitionSpec as P

GELU_SCALE = 0.7978845608
GELU_CUBIC = 0.044715
F32 = jnp.float32
BF16 = jnp.bfloat16
HIGHEST = lax.Precision.HIGHEST
MESH = pl.DeviceIdType.MESH
Z_TYPE = BF16
CELLS = 64 * 2048
OWN = 512
C0, C1 = 256, 512
W = 80


def gelu_value(z):
    return 0.5 * z * (1.0 + jnp.tanh(GELU_SCALE * (z + GELU_CUBIC * (z * z * z))))


def gelu_both(z):
    square = z * z
    hyper = jnp.tanh(GELU_SCALE * (z + GELU_CUBIC * (square * z)))
    half = 0.5 * (1.0 + hyper)
    slope = half + 0.5 * z * (1.0 - hyper * hyper) * GELU_SCALE * (1.0 + 3.0 * GELU_CUBIC * square)
    return z * half, slope


def flat(block):
    return block.reshape(block.shape[0] * block.shape[1], block.shape[2])


def dot_nn(left, right):
    return jnp.dot(left, right, preferred_element_type=F32)


def dot_nt(left, right):
    return lax.dot_general(left, right, (((1,), (1,)), ((), ())), preferred_element_type=F32)


def ahead(x, step):
    return x if step == 0 else pltpu.roll(x, (-step) % x.shape[0], 0)


def kernel(
    pool_hbm, w1_hbm, w2_hbm, tg_hbm, out,
    pool, w1, w2, tg, ts, pad, xs, pre1, act1, sl1, fsm, fs, act2m, act2, sl2,
    ch1, cl1, ch2, cl2, gs2, gs1, s0, r0, tsum, r1, means, dxs, zb, zm, ga, sh, sl, mean_ref,
    local_sem, halo_send, halo_recv, pair_send, pair_recv, rs_send, rs_recv,
    z_send, z_recv, ag_send, ag_recv, fw_send, fw_recv,
):
    g = lax.axis_index("grp")
    t = lax.axis_index("tile")
    core = lax.rem(t, 2)
    x_hi = lax.rem(t // 2, 2)
    z = t // 4
    k = x_hi * 8 + g
    strip = core * 16 + k

    partner = (g, z * 4 + x_hi * 2 + 1 - core)

    def xy_peer(other):
        return (lax.rem(other, 8), z * 4 + (other // 8) * 2 + core)

    def z_peer(other):
        return (g, other * 4 + x_hi * 2 + core)

    sides = [(i, j) for i in (-1, 0, 1) for j in (-1, 0, 1) if (i, j) != (0, 0)]

    def side_peer(i, j):
        return (lax.rem(g + i + 8, 8), lax.rem(t + j + 32, 32))

    loads = [
        pltpu.make_async_copy(source, target, local_sem.at[i])
        for i, (source, target) in enumerate(
            ((pool_hbm, pool), (tg_hbm, tg), (w1_hbm, w1), (w2_hbm, w2))
        )
    ]
    for load in loads:
        load.start()
    barrier = pltpu.get_barrier_semaphore()

    def greet(device):
        pl.semaphore_signal(barrier, inc=1, device_id=device, device_id_type=MESH)

    for i, j in sides:
        greet(side_peer(i, j))
    greet(partner)

    def greet_xy(i, carry):
        greet(xy_peer(lax.rem(k + i, 16)))
        return carry

    def greet_z(i, carry):
        greet(z_peer(lax.rem(z + i, 8)))
        return carry

    lax.fori_loop(1, 16, greet_xy, 0)
    lax.fori_loop(1, 8, greet_z, 0)
    loads[0].wait()
    pad[4:12, 16:80, :] = pool[...].astype(BF16)
    pl.semaphore_wait(barrier, 31)

    rows_from = {1: (8, 4), 0: (4, 8), -1: (4, 4)}
    rows_to = {1: (0, 4), 0: (4, 8), -1: (12, 4)}
    cols_from = {1: (64, 16), 0: (16, 64), -1: (16, 16)}
    cols_to = {1: (0, 16), 0: (16, 64), -1: (80, 16)}
    halos = []
    for n, (i, j) in enumerate(sides):
        (fr, nr), (fc, nc) = rows_from[i], cols_from[j]
        (tr, _), (tc, _) = rows_to[i], cols_to[j]
        halos.append(
            pltpu.make_async_remote_copy(
                src_ref=pad.at[pl.ds(fr, nr), pl.ds(fc, nc)],
                dst_ref=pad.at[pl.ds(tr, nr), pl.ds(tc, nc)],
                send_sem=halo_send.at[n],
                recv_sem=halo_recv.at[n],
                device_id=side_peer(i, j),
                device_id_type=MESH,
            )
        )
    for copy in halos:
        copy.start()

    loads[1].wait()
    for l in range(2):
        whole = tg[l]
        ts[l] = (whole + whole.T) * 0.5
    loads[2].wait()
    loads[3].wait()
    for copy in halos:
        copy.wait_recv()

    def clear_edges(ref, up, down, left, right):
        @pl.when(g == 0)
        def _():
            ref[0:up] = jnp.zeros((up, *ref.shape[1:]), ref.dtype)

        @pl.when(g == 7)
        def _():
            ref[ref.shape[0] - down :] = jnp.zeros((down, *ref.shape[1:]), ref.dtype)

        @pl.when(t == 0)
        def _():
            ref[:, 0:left] = jnp.zeros((ref.shape[0], left, ref.shape[2]), ref.dtype)

        @pl.when(t == 31)
        def _():
            ref[:, ref.shape[1] - right :] = jnp.zeros(
                (ref.shape[0], right, ref.shape[2]), ref.dtype
            )

    clear_edges(pad, 4, 4, 16, 16)

    def shift_pool(r, carry):
        x = pad[r].astype(F32)
        for b in range(3):
            xs[r, :, b * C0 : (b + 1) * C0] = ahead(x, b - 1)[8 : 8 + W].astype(BF16)
        return carry

    def conv1(first, rows):
        total = None
        for a in range(3):
            part = dot_nn(flat(xs[pl.ds(first + a, rows)]), w1[a])
            total = part if total is None else total + part
        pre1[pl.ds(first, rows)] = total.reshape(rows, W, C1)

    def gelu_row(r, carry):
        act1[r] = gelu_value(pre1[r])
        return carry

    lax.fori_loop(2, 14, shift_pool, 0)

    def conv1_step(i, carry):
        conv1(2 + 5 * i, 5)
        return carry

    lax.fori_loop(0, 2, conv1_step, 0)
    lax.fori_loop(2, 12, gelu_row, 0)
    clear_edges(act1.at[pl.ds(2, 10)], 1, 1, 8, 8)

    def shift_first(r, carry):
        x = act1[r + 2]
        for b in range(3):
            fsm[r, :, b * C1 : (b + 1) * C1] = ahead(x, b - 1)[8:72].astype(BF16)
        return carry

    lax.fori_loop(0, 10, shift_first, 0)

    def local_gram(l, x):
        mean = jnp.sum(x, axis=0, keepdims=True) * (1.0 / OWN)
        means[l, 2 * k + core] = mean
        cen = (x - mean).astype(BF16)
        gram = lax.dot_general(cen, cen, (((0,), (0,)), ((), ())), preferred_element_type=F32)
        for i in range(4):
            for d in range(3):
                j = (i + d) % 4
                block = gram[128 * i : 128 * i + 128, 128 * j : 128 * j + 128].astype(BF16)
                s0[l, i // 2, (i % 2) * 8 : (i % 2) * 8 + 8, :, 128 * d : 128 * d + 128] = (
                    block.reshape(8, 16, 128)
                )

    def pair_copies(l):
        return (
            pltpu.make_async_remote_copy(
                src_ref=s0.at[l, 1 - core],
                dst_ref=r0.at[l],
                send_sem=pair_send.at[l, 0],
                recv_sem=pair_recv.at[l, 0],
                device_id=partner,
                device_id_type=MESH,
            ),
            pltpu.make_async_remote_copy(
                src_ref=means.at[l, 2 * k + core],
                dst_ref=means.at[l, 2 * k + core],
                send_sem=pair_send.at[l, 1],
                recv_sem=pair_recv.at[l, 1],
                device_id=partner,
                device_id_type=MESH,
            ),
        )

    def rs_copies(l, to, slot):
        return (
            pltpu.make_async_remote_copy(
                src_ref=tsum.at[l, to],
                dst_ref=r1.at[l, slot],
                send_sem=rs_send.at[l, 0, to],
                recv_sem=rs_recv.at[l, 0, slot],
                device_id=xy_peer(to),
                device_id_type=MESH,
            ),
            pltpu.make_async_remote_copy(
                src_ref=means.at[l, pl.ds(2 * k, 2)],
                dst_ref=means.at[l, pl.ds(2 * slot, 2)],
                send_sem=rs_send.at[l, 1, to],
                recv_sem=rs_recv.at[l, 1, slot],
                device_id=xy_peer(to),
                device_id_type=MESH,
            ),
        )

    def pair_start(l):
        for copy in pair_copies(l):
            copy.start()

    def rs_start(l):
        for copy in pair_copies(l):
            copy.wait_recv()
        tsum[l] = (s0[l, core].astype(F32) + r0[l].astype(F32)).astype(BF16)
        r1[l, k] = tsum[l, k]

        def send(i, carry):
            for copy in rs_copies(l, lax.rem(k + i, 16), k):
                copy.start()
            return carry

        lax.fori_loop(1, 16, send, 0)

    def rs_wait(l):
        def wait(i, carry):
            other = lax.rem(k + 16 - i, 16)
            for copy in rs_copies(l, other, other):
                copy.wait_recv()
            return carry

        lax.fori_loop(1, 16, wait, 0)

    def spread(rows):
        mean = jnp.sum(rows, axis=0, keepdims=True) * (1.0 / rows.shape[0])
        off = rows - mean
        n = rows.shape[0]
        dxs[0:n, 0:C1] = off
        dxs[0:n, C1:] = off[:, 0:256]
        lane = lax.broadcasted_iota(jnp.int32, (16, C1), 1)
        sub = lax.broadcasted_iota(jnp.int32, (16, C1), 0)
        pick = jnp.where(lane == strip * 16 + sub, 1.0, 0.0).astype(F32)
        left = lax.dot_general(
            pick, off, (((1,), (1,)), ((), ())), precision=HIGHEST, preferred_element_type=F32
        )
        right = dxs[0:n, pl.ds(pl.multiple_of((strip // 8) * 128, 128), 384)]
        return mean, jnp.dot(left, right, precision=HIGHEST, preferred_element_type=F32)

    def z_copies(to, slot):
        return (
            pltpu.make_async_remote_copy(
                src_ref=zb.at[z],
                dst_ref=zb.at[slot],
                send_sem=z_send.at[0, to],
                recv_sem=z_recv.at[0, slot],
                device_id=z_peer(to),
                device_id_type=MESH,
            ),
            pltpu.make_async_remote_copy(
                src_ref=zm.at[z],
                dst_ref=zm.at[slot],
                send_sem=z_send.at[1, to],
                recv_sem=z_recv.at[1, slot],
                device_id=z_peer(to),
                device_id_type=MESH,
            ),
        )

    def ag_copy(to, slot):
        return pltpu.make_async_remote_copy(
            src_ref=ga.at[core, k],
            dst_ref=ga.at[core, slot],
            send_sem=ag_send.at[to],
            recv_sem=ag_recv.at[slot],
            device_id=xy_peer(to),
            device_id_type=MESH,
        )

    def fw_copy(side, slot):
        return pltpu.make_async_remote_copy(
            src_ref=ga.at[side, slot],
            dst_ref=ga.at[side, slot],
            send_sem=fw_send.at[slot],
            recv_sem=fw_recv.at[slot],
            device_id=partner,
            device_id_type=MESH,
        )

    local_gram(0, flat(act1[3:11, 8:72, :]))
    pair_start(0)

    def conv2_main(i, carry):
        total = None
        for a in range(3):
            part = dot_nn(flat(fsm[pl.ds(4 * i + a, 4)]), w2[a])
            total = part if total is None else total + part
        act2m[pl.ds(4 * i, 4)] = gelu_value(total).reshape(4, 64, C1)
        return carry

    lax.fori_loop(0, 1, conv2_main, 0)
    rs_start(0)
    lax.fori_loop(1, 2, conv2_main, 0)
    local_gram(1, flat(act2m[...]))
    pair_start(1)

    lax.fori_loop(0, 2, shift_pool, 0)
    lax.fori_loop(14, 16, shift_pool, 0)
    rs_start(1)

    def conv1_rim(i, carry):
        conv1(12 * i, 2)
        return carry

    lax.fori_loop(0, 2, conv1_rim, 0)

    def finish_first(r, carry):
        value, slope = gelu_both(pre1[r])
        act1[r] = value
        sl1[r] = slope
        return carry

    lax.fori_loop(0, 14, finish_first, 0)
    clear_edges(act1, 3, 3, 8, 8)
    clear_edges(sl1.at[pl.ds(2, 10)], 1, 1, 8, 8)

    def shift_first_all(r, carry):
        x = act1[r]
        for b in range(3):
            fs[r, :, b * C1 : (b + 1) * C1] = ahead(x, b - 1).astype(BF16)
        return carry

    lax.fori_loop(0, 14, shift_first_all, 0)

    rs_wait(0)
    rs_wait(1)
    for l in range(2):
        mean, extra = spread(means[l].reshape(32, C1))
        total = jnp.sum(r1[l].astype(F32), axis=0) + float(OWN) * extra
        zb[z, l] = total.astype(Z_TYPE)
        zm[z, l] = mean

    def z_send_step(i, carry):
        for copy in z_copies(lax.rem(z + i, 8), z):
            copy.start()
        return carry

    lax.fori_loop(1, 8, z_send_step, 0)

    def conv2_all(i, carry):
        total = None
        for a in range(3):
            part = dot_nn(flat(fs[pl.ds(4 * i + a, 4)]), w2[a])
            total = part if total is None else total + part
        value, slope = gelu_both(total)
        act2[pl.ds(4 * i, 4)] = value.reshape(4, W, C1)
        sl2[pl.ds(4 * i, 4)] = slope.reshape(4, W, C1)
        return carry

    lax.fori_loop(0, 2, conv2_all, 0)

    def z_wait_step(i, carry):
        other = lax.rem(z + 8 - i, 8)
        for copy in z_copies(other, other):
            copy.wait_recv()
        return carry

    lax.fori_loop(1, 8, z_wait_step, 0)
    for l in range(2):
        mean, extra = spread(zm[:, l].reshape(8, C1))
        total = jnp.sum(zb[:, l].astype(F32), axis=0) + float(32 * OWN) * extra
        mean_ref[l] = mean
        ga[core, k, l] = (total * (1.0 / CELLS)).astype(BF16)

    def ag_send_step(i, carry):
        ag_copy(lax.rem(k + i, 16), k).start()
        return carry

    lax.fori_loop(1, 16, ag_send_step, 0)
    fw_copy(core, k).start()

    lax.fori_loop(2, 3, conv2_all, 0)
    clear_edges(sl2, 2, 2, 8, 8)

    def ag_wait_step(i, carry):
        other = lax.rem(k + 16 - i, 16)
        ag_copy(other, other).wait_recv()
        fw_copy(core, other).start()
        return carry

    lax.fori_loop(1, 16, ag_wait_step, 0)

    def centre(source, high, low, mean, shift):
        def step(r, carry):
            cen = source[r + shift] - mean
            top = cen.astype(BF16)
            high[r] = top
            low[r] = (cen - top.astype(F32)).astype(BF16)
            return carry

        return step

    lax.fori_loop(0, 12, centre(act2, ch2, cl2, mean_ref[1], 0), 0)
    lax.fori_loop(0, 10, centre(act1, ch1, cl1, mean_ref[0], 2), 0)

    def fw_wait_step(slot, carry):
        fw_copy(1 - core, slot).wait_recv()
        return carry

    lax.fori_loop(0, 16, fw_wait_step, 0)

    def put(l, i, j, block):
        block = block - ts[l, 128 * i : 128 * i + 128, 128 * j : 128 * j + 128]
        top = block.astype(BF16)
        sh[l, 128 * i : 128 * i + 128, 128 * j : 128 * j + 128] = top
        sl[l, 128 * i : 128 * i + 128, 128 * j : 128 * j + 128] = (
            block - top.astype(F32)
        ).astype(BF16)

    for l in (1, 0):
        for i in range(4):
            strips = ga[i // 2, (i % 2) * 8 : (i % 2) * 8 + 8, l].astype(F32).reshape(128, 384)
            for d in range(3):
                block = strips[:, 128 * d : 128 * d + 128]
                put(l, i, (i + d) % 4, block)
                if d == 1:
                    put(l, (i + 1) % 4, i, block.T)

    def push(l, high, low, first, rows):
        top = flat(high[pl.ds(first, rows)])
        rest = flat(low[pl.ds(first, rows)])
        return dot_nn(top, sh[l]) + dot_nn(rest, sh[l]) + dot_nn(top, sl[l])

    def back2(i, carry):
        grad = push(1, ch2, cl2, 4 * i, 4) * flat(sl2[pl.ds(4 * i, 4)])
        for b in range(3):
            gs2[pl.ds(4 * i, 4), :, b * C1 : (b + 1) * C1] = (
                ahead(grad, 1 - b).astype(BF16).reshape(4, W, C1)
            )
        return carry

    lax.fori_loop(0, 3, back2, 0)

    def back1(i, carry):
        flow = push(0, ch1, cl1, 5 * i, 5)
        for a in range(3):
            for b in range(3):
                flow = flow + dot_nt(
                    flat(gs2[pl.ds(5 * i + 2 - a, 5), :, b * C1 : (b + 1) * C1]),
                    w2[a, b * C1 : (b + 1) * C1, :],
                )
        grad = flow * flat(sl1[pl.ds(5 * i + 2, 5)])
        for b in range(3):
            gs1[pl.ds(5 * i, 5), :, b * C1 : (b + 1) * C1] = (
                ahead(grad, 1 - b).reshape(5, W, C1)[:, 8:72].astype(BF16)
            )
        return carry

    lax.fori_loop(0, 2, back1, 0)

    def back0(i, carry):
        total = None
        for a in range(3):
            for b in range(3):
                part = dot_nt(
                    flat(gs1[pl.ds(4 * i + 2 - a, 4), :, b * C1 : (b + 1) * C1]),
                    w1[a, b * C0 : (b + 1) * C0, :],
                )
                total = part if total is None else total + part
        out[pl.ds(4 * i, 4)] = total.reshape(4, 64, C0)
        return carry

    lax.fori_loop(0, 2, back0, 0)

    for copy in halos:
        copy.wait_send()
    for l in range(2):
        for copy in pair_copies(l):
            copy.wait_send()

    def rs_drain(i, carry):
        for l in range(2):
            for copy in rs_copies(l, lax.rem(k + i, 16), k):
                copy.wait_send()
        ag_copy(lax.rem(k + i, 16), k).wait_send()
        return carry

    lax.fori_loop(1, 16, rs_drain, 0)

    def z_drain(i, carry):
        for copy in z_copies(lax.rem(z + i, 8), z):
            copy.wait_send()
        return carry

    lax.fori_loop(1, 8, z_drain, 0)

    def fw_drain(slot, carry):
        fw_copy(core, slot).wait_send()
        return carry

    lax.fori_loop(0, 16, fw_drain, 0)


def local(pool_input, weight_first, weight_second, targets):
    v = pltpu.VMEM
    dma = pltpu.SemaphoreType.DMA
    scratch = [
        v((8, 64, C0), F32),
        v((3, 3 * C0, C1), BF16),
        v((3, 3 * C1, C1), BF16),
        v((2, C1, C1), F32),
        v((2, C1, C1), F32),
        v((16, 96, C0), BF16),
        v((16, W, 3 * C0), BF16),
        v((14, W, C1), F32),
        v((14, W, C1), F32),
        v((14, W, C1), F32),
        v((10, 64, 3 * C1), BF16),
        v((14, W, 3 * C1), BF16),
        v((8, 64, C1), F32),
        v((12, W, C1), F32),
        v((12, W, C1), F32),
        v((10, W, C1), BF16),
        v((10, W, C1), BF16),
        v((12, W, C1), BF16),
        v((12, W, C1), BF16),
        v((12, W, 3 * C1), BF16),
        v((10, 64, 3 * C1), BF16),
        v((2, 2, 16, 16, 384), BF16),
        v((2, 16, 16, 384), BF16),
        v((2, 16, 16, 384), BF16),
        v((2, 16, 16, 384), BF16),
        v((2, 32, 1, C1), F32),
        v((32, C1 + 256), F32),
        v((8, 2, 16, 384), Z_TYPE),
        v((8, 2, 1, C1), F32),
        v((2, 16, 2, 16, 384), BF16),
        v((2, C1, C1), BF16),
        v((2, C1, C1), BF16),
        v((2, 1, C1), F32),
        dma((4,)),
        dma((8,)),
        dma((8,)),
        dma((2, 2)),
        dma((2, 2)),
        dma((2, 2, 16)),
        dma((2, 2, 16)),
        dma((2, 8)),
        dma((2, 8)),
        dma((16,)),
        dma((16,)),
        dma((16,)),
        dma((16,)),
    ]
    anywhere = pl.BlockSpec(memory_space=pl.ANY)
    return pl.pallas_call(
        kernel,
        out_shape=jax.ShapeDtypeStruct((8, 64, C0), F32),
        in_specs=[anywhere] * 4,
        out_specs=pl.BlockSpec(memory_space=pltpu.VMEM),
        scratch_shapes=scratch,
        compiler_params=pltpu.CompilerParams(
            collective_id=0, has_side_effects=True, vmem_limit_bytes=67043328
        ),
        name="style_grad",
    )(
        pool_input,
        weight_first.reshape(3, 3 * C0, C1),
        weight_second.reshape(3, 3 * C1, C1),
        targets,
    )


def solution(mesh):
    return jax.shard_map(
        local,
        mesh=mesh,
        in_specs=(P("grp", "tile", None), P(), P(), P()),
        out_specs=P("grp", "tile", None),
        check_vma=False,
    )
```

time: 303 us -> 67.4 us (0.22)
  the two profiles are of different devices: /device:TPU:152 before, /device:TPU:1 now
where the time goes in v1:
time: 67.4 us; the launch traced here: 67.3 us
  Pallas kernels  65.4 us (97%)
  local copies, waits for them, and re-layouts  1.87 us (3%)
    pallas_call x1, Pallas kernels, local(): pl.pallas_call(kernel, out_shape=jax.ShapeDtypeStruct((8, 64, C0), F32),...  65.4 us
    unnamed x1, local copies, waits for them, and re-layouts  1.87 us

profile of v1, /device:TPU:1, one launch (start us, length us, event | category | flops | bytes accessed | tf_op | source)
XLA Modules:
  0.0 67.3 jit_solution(1555960542184154415)
XLA Ops:
  0.0 65.4 %style_grad.1 = f32[8,64,256]{2,1,0:T(8,128)} custom-call(f32[8,64,256]{2,1,0:T(8,128)} %pool_hbm.1, bf16[3,768,512]{2,1,0:T(8,128)(2,1)} %bitcast.3, bf16[3,1536,512]{2,1,0:T(8,128)(2,1)} %bitcast.2, f32[2,512,512]{2,1,0:T(8,128)} %tg_hbm.1), custom_call_target="tpu_custom_call" | custom-call | tf_op jit(solution)/shard_map/style_grad/pallas_call | solution.py:596
  65.4 1.9 %copy.6 = f32[8,64,256]{2,1,0:T(8,128)} copy(f32[8,64,256]{2,1,0:T(8,128)} %style_grad.1) | data formatting | bytes 1048576

commit v2 on v1

v2 whole, which is shorter than its diff:
```python
import functools

import jax
import jax.numpy as jnp
from jax import lax
from jax.experimental import pallas as pl
from jax.experimental.pallas import tpu as pltpu
from jax.sharding import PartitionSpec as P

GELU_SCALE = 0.7978845608
GELU_CUBIC = 0.044715
F32 = jnp.float32
BF16 = jnp.bfloat16
HIGHEST = lax.Precision.HIGHEST
MESH = pl.DeviceIdType.MESH
Z_TYPE = BF16
CELLS = 64 * 2048
OWN = 512
C0, C1 = 256, 512
W = 80


def gelu_value(z):
    return 0.5 * z * (1.0 + jnp.tanh(GELU_SCALE * (z + GELU_CUBIC * (z * z * z))))


def gelu_both(z):
    square = z * z
    hyper = jnp.tanh(GELU_SCALE * (z + GELU_CUBIC * (square * z)))
    half = 0.5 * (1.0 + hyper)
    slope = half + 0.5 * z * (1.0 - hyper * hyper) * GELU_SCALE * (1.0 + 3.0 * GELU_CUBIC * square)
    return z * half, slope


def flat(block):
    return block.reshape(block.shape[0] * block.shape[1], block.shape[2])


def dot_nn(left, right):
    return jnp.dot(left, right, preferred_element_type=F32)


def dot_nt(left, right):
    return lax.dot_general(left, right, (((1,), (1,)), ((), ())), preferred_element_type=F32)


def ahead(x, step):
    return x if step == 0 else pltpu.roll(x, (-step) % x.shape[0], 0)


def kernel(
    pool_hbm, w1_hbm, w2_hbm, tg_hbm, out_hbm,
    pool, w1, w2, tg, ts, pad, xs, pre1, act1, sl1, fsm, fs, act2m, act2, sl2,
    ch1, cl1, ch2, cl2, s0, r0, tsum, r1, means, dxs, zb, zm, ga, sh, sl, outv,
    local_sem, halo_send, halo_recv, pair_send, pair_recv, rs_send, rs_recv,
    z_send, z_recv, ag_send, ag_recv, fw_send, fw_recv,
):
    gs1, gs2, flow1 = fsm, fs, pre1
    g = lax.axis_index("grp")
    t = lax.axis_index("tile")
    core = lax.rem(t, 2)
    x = lax.rem(t // 2, 2) * 2 + g // 4
    y = lax.rem(g, 4)
    z = t // 4
    k = x * 4 + y
    strip = core * 16 + k

    def device(x_to, y_to, z_to, core_to):
        return (lax.rem(x_to, 2) * 4 + y_to, z_to * 4 + (x_to // 2) * 2 + core_to)

    partner = device(x, y, z, 1 - core)

    def xy_peer(other):
        return device(other // 4, lax.rem(other, 4), z, core)

    def z_peer(other):
        return device(x, y, other, core)

    xy_steps = sorted(
        ((i, j) for i in range(4) for j in range(4) if (i, j) != (0, 0)),
        key=lambda s: -(min(s[0], 4 - s[0]) + min(s[1], 4 - s[1])),
    )
    xy_others = [lax.rem(x + i, 4) * 4 + lax.rem(y + j, 4) for i, j in xy_steps]
    z_others = [lax.rem(z + i, 8) for i in (4, 3, 5, 2, 6, 1, 7)]
    sides = [(i, j) for i in (-1, 1) for j in (-1, 1, 0)] + [(0, -1), (0, 1)]

    def side_peer(i, j):
        return (lax.rem(g + i + 8, 8), lax.rem(t + j + 32, 32))

    loads = [
        pltpu.make_async_copy(source, target, local_sem.at[i])
        for i, (source, target) in enumerate(
            ((pool_hbm, pool), (tg_hbm, tg), (w1_hbm, w1), (w2_hbm, w2))
        )
    ]
    for load in loads:
        load.start()
    barrier = pltpu.get_barrier_semaphore()

    def greet(who):
        pl.semaphore_signal(barrier, inc=1, device_id=who, device_id_type=MESH)

    for i, j in sides:
        greet(side_peer(i, j))
    for other in xy_others:
        greet(xy_peer(other))
    for other in z_others:
        greet(z_peer(other))
    greet(partner)
    loads[0].wait()
    pad[4:12, 1:9] = pool[...].astype(BF16).reshape(8, 8, 8, C0)
    pl.semaphore_wait(barrier, 31)

    cols_from = {1: (8, 1), 0: (1, 8), -1: (1, 1)}
    cols_to = {1: (0, 1), 0: (1, 8), -1: (9, 1)}

    def halo(n, i, j, row_from, row_to, rows):
        (fc, nc), (tc, _) = cols_from[j], cols_to[j]
        return pltpu.make_async_remote_copy(
            src_ref=pad.at[pl.ds(row_from, rows), pl.ds(fc, nc)],
            dst_ref=pad.at[pl.ds(row_to, rows), pl.ds(tc, nc)],
            send_sem=halo_send.at[n],
            recv_sem=halo_recv.at[n],
            device_id=side_peer(i, j),
            device_id_type=MESH,
        )

    near_rows = {1: (10, 2, 2), 0: (4, 4, 8), -1: (4, 12, 2)}
    far_rows = {1: (8, 0, 2), -1: (6, 14, 2)}
    near = [halo(n, i, j, *near_rows[i]) for n, (i, j) in enumerate(sides)]
    far = [halo(8 + n, i, j, *far_rows[i]) for n, (i, j) in enumerate(sides) if i != 0]
    for copy in near + far:
        copy.start()

    loads[1].wait()
    for l in range(2):
        whole = tg[l]
        ts[l] = (whole + whole.T) * 0.5
    loads[2].wait()
    loads[3].wait()
    for copy in near:
        copy.wait_recv()

    def on_edges(top, bottom, left, right):
        pl.when(g == 0)(top)
        pl.when(g == 7)(bottom)
        pl.when(t == 0)(left)
        pl.when(t == 31)(right)

    def clear_pad(up, down, blocks):
        def zero(first, rows, col, cols):
            pad[first : first + rows, col : col + cols] = jnp.zeros((rows, cols, 8, C0), BF16)

        def column(col):
            for first, rows in blocks:
                zero(first, rows, col, 1)

        on_edges(
            lambda: zero(up, 2, 0, 10),
            lambda: zero(down, 2, 0, 10),
            lambda: column(0),
            lambda: column(9),
        )

    def clear_edges(ref, first, rows, depth):
        def zero(row, n, col, cols):
            ref[row : row + n, col : col + cols] = jnp.zeros((n, cols, ref.shape[2]), ref.dtype)

        on_edges(
            lambda: zero(first, depth, 0, W),
            lambda: zero(first + rows - depth, depth, 0, W),
            lambda: zero(first, rows, 0, 8),
            lambda: zero(first, rows, W - 8, 8),
        )

    clear_pad(2, 12, ((2, 12),))

    def shift_pool(r, carry):
        row = pad[r].astype(F32).reshape(W, C0)
        for b in range(3):
            xs[r, :, b * C0 : (b + 1) * C0] = ahead(row, b - 1).astype(BF16)
        return carry

    def conv1(first, rows):
        total = None
        for a in range(3):
            part = dot_nn(flat(xs[pl.ds(first + a, rows)]), w1[a])
            total = part if total is None else total + part
        pre1[pl.ds(first, rows)] = total.reshape(rows, W, C1)

    def gelu_row(r, carry):
        act1[r] = gelu_value(pre1[r])
        return carry

    lax.fori_loop(2, 14, shift_pool, 0)

    def conv1_step(i, carry):
        conv1(2 + 5 * i, 5)
        return carry

    lax.fori_loop(0, 2, conv1_step, 0)
    lax.fori_loop(2, 12, gelu_row, 0)
    clear_edges(act1, 2, 10, 1)

    def shift_first(r, carry):
        row = act1[r + 2]
        for b in range(3):
            fsm[r, :, b * C1 : (b + 1) * C1] = ahead(row, b - 1)[8:72].astype(BF16)
        return carry

    lax.fori_loop(0, 10, shift_first, 0)

    def remote(source, target, send, recv, who):
        return pltpu.make_async_remote_copy(
            src_ref=source, dst_ref=target, send_sem=send, recv_sem=recv,
            device_id=who, device_id_type=MESH,
        )

    def pair_piece(l):
        return remote(
            s0.at[l, 1 - core], r0.at[l], pair_send.at[l, 0], pair_recv.at[l, 0], partner
        )

    def pair_mean(l):
        own = means.at[l, 2 * k + core]
        return remote(own, own, pair_send.at[l, 1], pair_recv.at[l, 1], partner)

    def pair_mean_in(l):
        other = means.at[l, 2 * k + 1 - core]
        return remote(other, other, pair_send.at[l, 1], pair_recv.at[l, 1], partner)

    def rs_piece(l, to, slot):
        return remote(
            tsum.at[l, to], r1.at[l, slot], rs_send.at[l, 0, to], rs_recv.at[l, 0, slot], xy_peer(to)
        )

    def rs_mean(l, to, slot):
        both = means.at[l, pl.ds(2 * slot, 2)]
        return remote(both, both, rs_send.at[l, 1, to], rs_recv.at[l, 1, slot], xy_peer(to))

    def z_piece(l, to, slot):
        part = zb.at[l, slot]
        return remote(part, part, z_send.at[l, 0, to], z_recv.at[l, 0, slot], z_peer(to))

    def z_mean(l, to, slot):
        part = zm.at[l, slot]
        return remote(part, part, z_send.at[l, 1, to], z_recv.at[l, 1, slot], z_peer(to))

    def ag_piece(l, to, slot):
        part = ga.at[l, core, slot]
        return remote(part, part, ag_send.at[l, to], ag_recv.at[l, slot], xy_peer(to))

    def fw_piece(l, side, slot):
        part = ga.at[l, side, slot]
        return remote(part, part, fw_send.at[l, slot], fw_recv.at[l, slot], partner)

    def xy_wait(make, l):
        def step(i, carry):
            other = lax.rem(k + 16 - i, 16)
            make(l, other, other).wait_recv()
            return carry

        lax.fori_loop(1, 16, step, 0)

    def z_wait(make, l):
        def step(i, carry):
            other = lax.rem(z + 8 - i, 8)
            make(l, other, other).wait_recv()
            return carry

        lax.fori_loop(1, 8, step, 0)

    def local_gram(l, values):
        mean = jnp.sum(values, axis=0, keepdims=True) * (1.0 / OWN)
        means[l, 2 * k + core] = mean
        cen = (values - mean).astype(BF16)
        pair_mean(l).start()
        gram = lax.dot_general(cen, cen, (((0,), (0,)), ((), ())), preferred_element_type=F32)
        for i in range(4):
            for d in range(3):
                j = (i + d) % 4
                block = gram[128 * i : 128 * i + 128, 128 * j : 128 * j + 128].astype(BF16)
                s0[l, i // 2, (i % 2) * 8 : (i % 2) * 8 + 8, :, 128 * d : 128 * d + 128] = (
                    block.reshape(8, 16, 128)
                )
        pair_piece(l).start()

    def rs_start(l):
        pair_mean_in(l).wait_recv()
        for other in xy_others:
            rs_mean(l, other, k).start()
        pair_piece(l).wait_recv()
        tsum[l] = (s0[l, core].astype(F32) + r0[l].astype(F32)).astype(BF16)
        r1[l, k] = tsum[l, k]
        for other in xy_others:
            rs_piece(l, other, k).start()

    def spread(rows):
        n = rows.shape[0]
        mean = jnp.sum(rows, axis=0, keepdims=True) * (1.0 / n)
        off = rows - mean
        dxs[0:n, 0:C1] = off
        dxs[0:n, C1:] = off[:, 0:256]
        lane = lax.broadcasted_iota(jnp.int32, (16, C1), 1)
        sub = lax.broadcasted_iota(jnp.int32, (16, C1), 0)
        pick = jnp.where(lane == strip * 16 + sub, 1.0, 0.0).astype(F32)
        left = lax.dot_general(
            pick, off, (((1,), (1,)), ((), ())), precision=HIGHEST, preferred_element_type=F32
        )
        right = dxs[0:n, pl.ds(pl.multiple_of((strip // 8) * 128, 128), 384)]
        return mean, jnp.dot(left, right, precision=HIGHEST, preferred_element_type=F32)

    def plane_done(l):
        xy_wait(rs_mean, l)
        mean, extra = spread(means[l].reshape(32, C1))
        zm[l, z] = mean
        xy_wait(rs_piece, l)
        total = jnp.sum(r1[l].astype(F32), axis=0) + float(OWN) * extra
        zb[l, z] = total.astype(Z_TYPE)
        for other in z_others:
            z_mean(l, other, z).start()
        for other in z_others:
            z_piece(l, other, z).start()

    def z_done(l):
        z_wait(z_mean, l)
        mean, extra = spread(zm[l].reshape(8, C1))
        z_wait(z_piece, l)
        total = jnp.sum(zb[l].astype(F32), axis=0) + float(32 * OWN) * extra
        ga[l, core, k] = (total * (1.0 / CELLS)).astype(BF16)
        for other in xy_others:
            ag_piece(l, other, k).start()
        fw_piece(l, core, k).start()
        return mean

    def gathered(l):
        def step(i, carry):
            other = lax.rem(k + 16 - i, 16)
            ag_piece(l, other, other).wait_recv()
            fw_piece(l, core, other).start()
            return carry

        lax.fori_loop(1, 16, step, 0)

    def forwarded(l):
        def step(slot, carry):
            fw_piece(l, 1 - core, slot).wait_recv()
            return carry

        lax.fori_loop(0, 16, step, 0)

    def mismatch(l):
        def put(i, j, block):
            block = block - ts[l, 128 * i : 128 * i + 128, 128 * j : 128 * j + 128]
            top = block.astype(BF16)
            sh[l, 128 * i : 128 * i + 128, 128 * j : 128 * j + 128] = top
            sl[l, 128 * i : 128 * i + 128, 128 * j : 128 * j + 128] = (
                block - top.astype(F32)
            ).astype(BF16)

        for i in range(4):
            rows = ga[l, i // 2, (i % 2) * 8 : (i % 2) * 8 + 8].astype(F32).reshape(128, 384)
            for d in range(3):
                block = rows[:, 128 * d : 128 * d + 128]
                put(i, (i + d) % 4, block)
                if d == 1:
                    put((i + 1) % 4, i, block.T)

    local_gram(0, flat(act1[3:11, 8:72, :]))

    def conv2_main(i, carry):
        total = None
        for a in range(3):
            part = dot_nn(flat(fsm[pl.ds(4 * i + a, 4)]), w2[a])
            total = part if total is None else total + part
        act2m[pl.ds(4 * i, 4)] = gelu_value(total).reshape(4, 64, C1)
        return carry

    lax.fori_loop(0, 1, conv2_main, 0)
    rs_start(0)
    lax.fori_loop(1, 2, conv2_main, 0)
    local_gram(1, flat(act2m[...]))

    for copy in far:
        copy.wait_recv()
    clear_pad(0, 14, ((0, 2), (14, 2)))
    lax.fori_loop(0, 2, shift_pool, 0)
    lax.fori_loop(14, 16, shift_pool, 0)

    def conv1_rim(i, carry):
        conv1(12 * i, 2)
        return carry

    lax.fori_loop(0, 2, conv1_rim, 0)
    rs_start(1)

    plane_done(0)

    def finish_first(r, carry):
        value, slope = gelu_both(pre1[r])
        act1[r] = value
        sl1[r] = slope
        return carry

    lax.fori_loop(0, 14, finish_first, 0)
    clear_edges(act1, 0, 14, 3)
    clear_edges(sl1, 2, 10, 1)

    def shift_first_all(r, carry):
        row = act1[r]
        for b in range(3):
            fs[r, :, b * C1 : (b + 1) * C1] = ahead(row, b - 1).astype(BF16)
        return carry

    lax.fori_loop(0, 14, shift_first_all, 0)

    plane_done(1)

    def conv2_all(i, carry):
        total = None
        for a in range(3):
            part = dot_nn(flat(fs[pl.ds(4 * i + a, 4)]), w2[a])
            total = part if total is None else total + part
        value, slope = gelu_both(total)
        act2[pl.ds(4 * i, 4)] = value.reshape(4, W, C1)
        sl2[pl.ds(4 * i, 4)] = slope.reshape(4, W, C1)
        return carry

    lax.fori_loop(0, 1, conv2_all, 0)
    mean_first = z_done(0)
    lax.fori_loop(1, 2, conv2_all, 0)
    mean_second = z_done(1)
    lax.fori_loop(2, 3, conv2_all, 0)
    clear_edges(sl2, 0, 12, 2)

    def centre(source, high, low, mean, shift):
        def step(r, carry):
            cen = source[r + shift] - mean
            top = cen.astype(BF16)
            high[r] = top
            low[r] = (cen - top.astype(F32)).astype(BF16)
            return carry

        return step

    lax.fori_loop(0, 10, centre(act1, ch1, cl1, mean_first, 2), 0)
    lax.fori_loop(0, 12, centre(act2, ch2, cl2, mean_second, 0), 0)

    def push(l, high, low, first, rows):
        top = flat(high[pl.ds(first, rows)])
        rest = flat(low[pl.ds(first, rows)])
        return dot_nn(top, sh[l]) + dot_nn(rest, sh[l]) + dot_nn(top, sl[l])

    gathered(0)
    forwarded(0)
    mismatch(0)

    def push_first(i, carry):
        flow1[pl.ds(5 * i, 5)] = push(0, ch1, cl1, 5 * i, 5).reshape(5, W, C1)
        return carry

    lax.fori_loop(0, 2, push_first, 0)

    gathered(1)

    for copy in near + far:
        copy.wait_send()
    for l in range(2):
        pair_piece(l).wait_send()
        pair_mean(l).wait_send()

    def rs_drain(i, carry):
        for l in range(2):
            rs_piece(l, lax.rem(k + i, 16), k).wait_send()
            rs_mean(l, lax.rem(k + i, 16), k).wait_send()
        return carry

    lax.fori_loop(1, 16, rs_drain, 0)

    def z_drain(i, carry):
        for l in range(2):
            z_piece(l, lax.rem(z + i, 8), z).wait_send()
            z_mean(l, lax.rem(z + i, 8), z).wait_send()
        return carry

    lax.fori_loop(1, 8, z_drain, 0)
    forwarded(1)

    mismatch(1)

    def back2(i, carry):
        grad = push(1, ch2, cl2, 4 * i, 4) * flat(sl2[pl.ds(4 * i, 4)])
        for b in range(3):
            gs2[pl.ds(4 * i, 4), :, b * C1 : (b + 1) * C1] = (
                ahead(grad, 1 - b).astype(BF16).reshape(4, W, C1)
            )
        return carry

    lax.fori_loop(0, 3, back2, 0)

    def back1(i, carry):
        flow = flat(flow1[pl.ds(5 * i, 5)])
        for a in range(3):
            for b in range(3):
                flow = flow + dot_nt(
                    flat(gs2[pl.ds(5 * i + 2 - a, 5), :, b * C1 : (b + 1) * C1]),
                    w2[a, b * C1 : (b + 1) * C1, :],
                )
        grad = flow * flat(sl1[pl.ds(5 * i + 2, 5)])
        for b in range(3):
            gs1[pl.ds(5 * i, 5), :, b * C1 : (b + 1) * C1] = (
                ahead(grad, 1 - b).reshape(5, W, C1)[:, 8:72].astype(BF16)
            )
        return carry

    lax.fori_loop(0, 2, back1, 0)

    def out_copy(i):
        rows = pl.ds(4 * i, 4)
        return pltpu.make_async_copy(outv.at[rows], out_hbm.at[rows], local_sem.at[i])

    def back0(i, carry):
        total = None
        for a in range(3):
            for b in range(3):
                part = dot_nt(
                    flat(gs1[pl.ds(4 * i + 2 - a, 4), :, b * C1 : (b + 1) * C1]),
                    w1[a, b * C0 : (b + 1) * C0, :],
                )
                total = part if total is None else total + part
        outv[pl.ds(4 * i, 4)] = total.reshape(4, 64, C0)
        out_copy(i).start()
        return carry

    lax.fori_loop(0, 2, back0, 0)

    def ag_drain(i, carry):
        for l in range(2):
            ag_piece(l, lax.rem(k + i, 16), k).wait_send()
        return carry

    lax.fori_loop(1, 16, ag_drain, 0)

    def fw_drain(slot, carry):
        for l in range(2):
            fw_piece(l, core, slot).wait_send()
        return carry

    lax.fori_loop(0, 16, fw_drain, 0)
    for i in range(2):
        out_copy(i).wait()


def local(pool_input, weight_first, weight_second, targets):
    v = pltpu.VMEM
    dma = pltpu.SemaphoreType.DMA
    scratch = [
        v((8, 64, C0), F32),
        v((3, 3 * C0, C1), BF16),
        v((3, 3 * C1, C1), BF16),
        v((2, C1, C1), F32),
        v((2, C1, C1), F32),
        v((16, 10, 8, C0), BF16),
        v((16, W, 3 * C0), BF16),
        v((14, W, C1), F32),
        v((14, W, C1), F32),
        v((14, W, C1), F32),
        v((10, 64, 3 * C1), BF16),
        v((14, W, 3 * C1), BF16),
        v((8, 64, C1), F32),
        v((12, W, C1), F32),
        v((12, W, C1), F32),
        v((10, W, C1), BF16),
        v((10, W, C1), BF16),
        v((12, W, C1), BF16),
        v((12, W, C1), BF16),
        v((2, 2, 16, 16, 384), BF16),
        v((2, 16, 16, 384), BF16),
        v((2, 16, 16, 384), BF16),
        v((2, 16, 16, 384), BF16),
        v((2, 32, 1, C1), F32),
        v((32, C1 + 256), F32),
        v((2, 8, 16, 384), Z_TYPE),
        v((2, 8, 1, C1), F32),
        v((2, 2, 16, 16, 384), BF16),
        v((2, C1, C1), BF16),
        v((2, C1, C1), BF16),
        v((8, 64, C0), F32),
        dma((4,)),
        dma((16,)),
        dma((16,)),
        dma((2, 2)),
        dma((2, 2)),
        dma((2, 2, 16)),
        dma((2, 2, 16)),
        dma((2, 2, 8)),
        dma((2, 2, 8)),
        dma((2, 16)),
        dma((2, 16)),
        dma((2, 16)),
        dma((2, 16)),
    ]
    anywhere = pl.BlockSpec(memory_space=pl.ANY)
    return pl.pallas_call(
        kernel,
        out_shape=jax.ShapeDtypeStruct((8, 64, C0), F32),
        in_specs=[pl.BlockSpec(memory_space=pltpu.HBM)] * 4,
        out_specs=anywhere,
        scratch_shapes=scratch,
        compiler_params=pltpu.CompilerParams(
            collective_id=0, has_side_effects=True, vmem_limit_bytes=56 * 1024 * 1024
        ),
        name="style_grad",
    )(
        pool_input,
        weight_first.reshape(3, 3 * C0, C1),
        weight_second.reshape(3, 3 * C1, C1),
        targets,
    )


def solution(mesh):
    return jax.shard_map(
        local,
        mesh=mesh,
        in_specs=(P("grp", "tile", None), P(), P(), P()),
        out_specs=P("grp", "tile", None),
        check_vma=False,
    )
```

time: 67.4 us -> 57.9 us (0.86)
  Pallas kernels: 65.4 us -> 55.9 us
    pallas_call x1, Pallas kernels: 65.4 us -> 55.9 us  [local(): pl.pallas_call(kernel, out_shape=jax.ShapeDtypeStruct((8, 64, C0), F32),...]
where the time goes in v2:
time: 57.9 us; the launch traced here: 57.8 us
  Pallas kernels  55.9 us (97%)
  local copies, waits for them, and re-layouts  1.87 us (3%)
    pallas_call x1, Pallas kernels, local(): pl.pallas_call(kernel, out_shape=jax.ShapeDtypeStruct((8, 64, C0), F32),...  55.9 us
    unnamed x1, local copies, waits for them, and re-layouts  1.87 us

profile of v2, /device:TPU:1, one launch (start us, length us, event | category | flops | bytes accessed | tf_op | source)
XLA Modules:
  0.0 57.8 jit_solution(1854040291136530864)
XLA Ops:
  0.0 55.9 %style_grad.1 = f32[8,64,256]{2,1,0:T(8,128)} custom-call(f32[8,64,256]{2,1,0:T(8,128)} %pool_hbm.1, bf16[3,768,512]{2,1,0:T(8,128)(2,1)} %bitcast.3, bf16[3,1536,512]{2,1,0:T(8,128)(2,1)} %bitcast.2, f32[2,512,512]{2,1,0:T(8,128)} %tg_hbm.1), custom_call_target="tpu_custom_call" | custom-call | tf_op jit(solution)/shard_map/style_grad/pallas_call | solution.py:604
  55.9 1.9 %copy.6 = f32[8,64,256]{2,1,0:T(8,128)} copy(f32[8,64,256]{2,1,0:T(8,128)} %style_grad.1) | data formatting | bytes 1048576

commit v3 on v2

--- a/solution.py
+++ b/solution.py
@@ -49,11 +49,10 @@
 
 
 def kernel(
-    pool_hbm, w1_hbm, w2_hbm, tg_hbm, out_hbm,
+    pool_hbm, w1_hbm, w2_hbm, tg_hbm, out,
     pool, w1, w2, tg, ts, pad, xs, pre1, act1, sl1, fsm, fs, act2m, act2, sl2,
-    ch1, cl1, ch2, cl2, s0, r0, tsum, r1, means, dxs, zb, zm, ga, sh, sl, outv,
-    local_sem, halo_send, halo_recv, pair_send, pair_recv, rs_send, rs_recv,
-    z_send, z_recv, ag_send, ag_recv, fw_send, fw_recv,
+    ch1, cl1, ch2, cl2, s0, r0, tsum, r1, means, dxs, zb, zm, ga, sh, sl,
+    local_sem, halo_sem, pair_send, pair_recv, rs_sem, z_sem, ag_send, ag_recv, fw_sem,
 ):
     gs1, gs2, flow1 = fsm, fs, pre1
     g = lax.axis_index("grp")
@@ -81,6 +80,8 @@
         key=lambda s: -(min(s[0], 4 - s[0]) + min(s[1], 4 - s[1])),
     )
     xy_others = [lax.rem(x + i, 4) * 4 + lax.rem(y + j, 4) for i, j in xy_steps]
+    xy_from = [lax.rem(x + 4 - i, 4) * 4 + lax.rem(y + 4 - j, 4) for i, j in xy_steps]
+    ag_order = range(15)
     z_others = [lax.rem(z + i, 8) for i in (4, 3, 5, 2, 6, 1, 7)]
     sides = [(i, j) for i in (-1, 1) for j in (-1, 1, 0)] + [(0, -1), (0, 1)]
 
@@ -114,23 +115,26 @@
     cols_from = {1: (8, 1), 0: (1, 8), -1: (1, 1)}
     cols_to = {1: (0, 1), 0: (1, 8), -1: (9, 1)}
 
-    def halo(n, i, j, row_from, row_to, rows):
+    def halo(i, j, row_from, row_to, rows, arrival):
         (fc, nc), (tc, _) = cols_from[j], cols_to[j]
         return pltpu.make_async_remote_copy(
             src_ref=pad.at[pl.ds(row_from, rows), pl.ds(fc, nc)],
             dst_ref=pad.at[pl.ds(row_to, rows), pl.ds(tc, nc)],
-            send_sem=halo_send.at[n],
-            recv_sem=halo_recv.at[n],
+            send_sem=halo_sem.at[0],
+            recv_sem=halo_sem.at[arrival],
             device_id=side_peer(i, j),
             device_id_type=MESH,
         )
 
     near_rows = {1: (10, 2, 2), 0: (4, 4, 8), -1: (4, 12, 2)}
     far_rows = {1: (8, 0, 2), -1: (6, 14, 2)}
-    near = [halo(n, i, j, *near_rows[i]) for n, (i, j) in enumerate(sides)]
-    far = [halo(8 + n, i, j, *far_rows[i]) for n, (i, j) in enumerate(sides) if i != 0]
+    near = [halo(i, j, *near_rows[i], 1) for i, j in sides]
+    far = [halo(i, j, *far_rows[i], 2) for i, j in sides if i != 0]
     for copy in near + far:
         copy.start()
+
+    def wait_all(part, sem):
+        pltpu.make_async_copy(part, part, sem).wait()
 
     loads[1].wait()
     for l in range(2):
@@ -138,8 +142,7 @@
         ts[l] = (whole + whole.T) * 0.5
     loads[2].wait()
     loads[3].wait()
-    for copy in near:
-        copy.wait_recv()
+    wait_all(pad.at[pl.ds(0, 7), pl.ds(0, 8)], halo_sem.at[1])
 
     def on_edges(top, bottom, left, right):
         pl.when(g == 0)(top)
@@ -229,46 +232,32 @@
         other = means.at[l, 2 * k + 1 - core]
         return remote(other, other, pair_send.at[l, 1], pair_recv.at[l, 1], partner)
 
-    def rs_piece(l, to, slot):
+    def rs_piece(l, other):
         return remote(
-            tsum.at[l, to], r1.at[l, slot], rs_send.at[l, 0, to], rs_recv.at[l, 0, slot], xy_peer(to)
-        )
-
-    def rs_mean(l, to, slot):
-        both = means.at[l, pl.ds(2 * slot, 2)]
-        return remote(both, both, rs_send.at[l, 1, to], rs_recv.at[l, 1, slot], xy_peer(to))
-
-    def z_piece(l, to, slot):
-        part = zb.at[l, slot]
-        return remote(part, part, z_send.at[l, 0, to], z_recv.at[l, 0, slot], z_peer(to))
-
-    def z_mean(l, to, slot):
-        part = zm.at[l, slot]
-        return remote(part, part, z_send.at[l, 1, to], z_recv.at[l, 1, slot], z_peer(to))
-
-    def ag_piece(l, to, slot):
+            tsum.at[l, other], r1.at[l, k], rs_sem.at[l, 0, 0], rs_sem.at[l, 0, 1], xy_peer(other)
+        )
+
+    def rs_mean(l, other):
+        both = means.at[l, pl.ds(2 * k, 2)]
+        return remote(both, both, rs_sem.at[l, 1, 0], rs_sem.at[l, 1, 1], xy_peer(other))
+
+    def z_piece(l, other):
+        part = zb.at[l, z]
+        return remote(part, part, z_sem.at[l, 0, 0], z_sem.at[l, 0, 1], z_peer(other))
+
+    def z_mean(l, other):
+        part = zm.at[l, z]
+        return remote(part, part, z_sem.at[l, 1, 0], z_sem.at[l, 1, 1], z_peer(other))
+
+    def ag_piece(l, n):
+        part = ga.at[l, core, k]
+        return remote(
+            part, part, ag_send.at[l], ag_recv.at[l, n // 4], xy_peer(xy_others[n])
+        )
+
+    def fw_piece(l, slot):
         part = ga.at[l, core, slot]
-        return remote(part, part, ag_send.at[l, to], ag_recv.at[l, slot], xy_peer(to))
-
-    def fw_piece(l, side, slot):
-        part = ga.at[l, side, slot]
-        return remote(part, part, fw_send.at[l, slot], fw_recv.at[l, slot], partner)
-
-    def xy_wait(make, l):
-        def step(i, carry):
-            other = lax.rem(k + 16 - i, 16)
-            make(l, other, other).wait_recv()
-            return carry
-
-        lax.fori_loop(1, 16, step, 0)
-
-    def z_wait(make, l):
-        def step(i, carry):
-            other = lax.rem(z + 8 - i, 8)
-            make(l, other, other).wait_recv()
-            return carry
-
-        lax.fori_loop(1, 8, step, 0)
+        return remote(part, part, fw_sem.at[l, 0], fw_sem.at[l, 1], partner)
 
     def local_gram(l, values):
         mean = jnp.sum(values, axis=0, keepdims=True) * (1.0 / OWN)
@@ -288,12 +277,12 @@
     def rs_start(l):
         pair_mean_in(l).wait_recv()
         for other in xy_others:
-            rs_mean(l, other, k).start()
+            rs_mean(l, other).start()
         pair_piece(l).wait_recv()
         tsum[l] = (s0[l, core].astype(F32) + r0[l].astype(F32)).astype(BF16)
         r1[l, k] = tsum[l, k]
         for other in xy_others:
-            rs_piece(l, other, k).start()
+            rs_piece(l, other).start()
 
     def spread(rows):
         n = rows.shape[0]
@@ -311,43 +300,36 @@
         return mean, jnp.dot(left, right, precision=HIGHEST, preferred_element_type=F32)
 
     def plane_done(l):
-        xy_wait(rs_mean, l)
+        wait_all(means.at[l, pl.ds(0, 30)], rs_sem.at[l, 1, 1])
         mean, extra = spread(means[l].reshape(32, C1))
         zm[l, z] = mean
-        xy_wait(rs_piece, l)
+        wait_all(r1.at[l, pl.ds(0, 15)], rs_sem.at[l, 0, 1])
         total = jnp.sum(r1[l].astype(F32), axis=0) + float(OWN) * extra
         zb[l, z] = total.astype(Z_TYPE)
         for other in z_others:
-            z_mean(l, other, z).start()
+            z_mean(l, other).start()
         for other in z_others:
-            z_piece(l, other, z).start()
+            z_piece(l, other).start()
 
     def z_done(l):
-        z_wait(z_mean, l)
+        wait_all(zm.at[l, pl.ds(0, 7)], z_sem.at[l, 1, 1])
         mean, extra = spread(zm[l].reshape(8, C1))
-        z_wait(z_piece, l)
+        wait_all(zb.at[l, pl.ds(0, 7)], z_sem.at[l, 0, 1])
         total = jnp.sum(zb[l].astype(F32), axis=0) + float(32 * OWN) * extra
         ga[l, core, k] = (total * (1.0 / CELLS)).astype(BF16)
-        for other in xy_others:
-            ag_piece(l, other, k).start()
-        fw_piece(l, core, k).start()
+        for n in ag_order:
+            ag_piece(l, n).start()
+        fw_piece(l, k).start()
         return mean
 
     def gathered(l):
-        def step(i, carry):
-            other = lax.rem(k + 16 - i, 16)
-            ag_piece(l, other, other).wait_recv()
-            fw_piece(l, core, other).start()
-            return carry
-
-        lax.fori_loop(1, 16, step, 0)
+        for n in ag_order:
+            if n % 4 == 0:
+                wait_all(ga.at[l, core, pl.ds(0, min(4, 15 - n))], ag_recv.at[l, n // 4])
+            fw_piece(l, xy_from[n]).start()
 
     def forwarded(l):
-        def step(slot, carry):
-            fw_piece(l, 1 - core, slot).wait_recv()
-            return carry
-
-        lax.fori_loop(0, 16, step, 0)
+        wait_all(ga.at[l, 1 - core], fw_sem.at[l, 1])
 
     def mismatch(l):
         def put(i, j, block):
@@ -381,8 +363,7 @@
     lax.fori_loop(1, 2, conv2_main, 0)
     local_gram(1, flat(act2m[...]))
 
-    for copy in far:
-        copy.wait_recv()
+    wait_all(pad.at[pl.ds(0, 5), pl.ds(0, 8)], halo_sem.at[2])
     clear_pad(0, 14, ((0, 2), (14, 2)))
     lax.fori_loop(0, 2, shift_pool, 0)
     lax.fori_loop(14, 16, shift_pool, 0)
@@ -451,39 +432,24 @@
         rest = flat(low[pl.ds(first, rows)])
         return dot_nn(top, sh[l]) + dot_nn(rest, sh[l]) + dot_nn(top, sl[l])
 
-    gathered(0)
-    forwarded(0)
-    mismatch(0)
-
     def push_first(i, carry):
         flow1[pl.ds(5 * i, 5)] = push(0, ch1, cl1, 5 * i, 5).reshape(5, W, C1)
         return carry
 
-    lax.fori_loop(0, 2, push_first, 0)
-
-    gathered(1)
-
-    for copy in near + far:
-        copy.wait_send()
+    gathered(0)
+    wait_all(pad.at[pl.ds(0, 12), pl.ds(0, 8)], halo_sem.at[0])
     for l in range(2):
         pair_piece(l).wait_send()
         pair_mean(l).wait_send()
-
-    def rs_drain(i, carry):
-        for l in range(2):
-            rs_piece(l, lax.rem(k + i, 16), k).wait_send()
-            rs_mean(l, lax.rem(k + i, 16), k).wait_send()
-        return carry
-
-    lax.fori_loop(1, 16, rs_drain, 0)
-
-    def z_drain(i, carry):
-        for l in range(2):
-            z_piece(l, lax.rem(z + i, 8), z).wait_send()
-            z_mean(l, lax.rem(z + i, 8), z).wait_send()
-        return carry
-
-    lax.fori_loop(1, 8, z_drain, 0)
+        wait_all(r1.at[l, pl.ds(0, 15)], rs_sem.at[l, 0, 0])
+        wait_all(means.at[l, pl.ds(0, 30)], rs_sem.at[l, 1, 0])
+        wait_all(zb.at[l, pl.ds(0, 7)], z_sem.at[l, 0, 0])
+        wait_all(zm.at[l, pl.ds(0, 7)], z_sem.at[l, 1, 0])
+    forwarded(0)
+    mismatch(0)
+    lax.fori_loop(0, 1, push_first, 0)
+    gathered(1)
+    lax.fori_loop(1, 2, push_first, 0)
     forwarded(1)
 
     mismatch(1)
@@ -515,9 +481,9 @@
 
     lax.fori_loop(0, 2, back1, 0)
 
-    def out_copy(i):
-        rows = pl.ds(4 * i, 4)
-        return pltpu.make_async_copy(outv.at[rows], out_hbm.at[rows], local_sem.at[i])
+    for l in range(2):
+        wait_all(ga.at[l, core, pl.ds(0, 15)], ag_send.at[l])
+        wait_all(ga.at[l, core], fw_sem.at[l, 0])
 
     def back0(i, carry):
         total = None
@@ -528,27 +494,10 @@
                     w1[a, b * C0 : (b + 1) * C0, :],
                 )
                 total = part if total is None else total + part
-        outv[pl.ds(4 * i, 4)] = total.reshape(4, 64, C0)
-        out_copy(i).start()
+        out[pl.ds(4 * i, 4)] = total.reshape(4, 64, C0)
         return carry
 
     lax.fori_loop(0, 2, back0, 0)
-
-    def ag_drain(i, carry):
-        for l in range(2):
-            ag_piece(l, lax.rem(k + i, 16), k).wait_send()
-        return carry
-
-    lax.fori_loop(1, 16, ag_drain, 0)
-
-    def fw_drain(slot, carry):
-        for l in range(2):
-            fw_piece(l, core, slot).wait_send()
-        return carry
-
-    lax.fori_loop(0, 16, fw_drain, 0)
-    for i in range(2):
-        out_copy(i).wait()
 
 
 def local(pool_input, weight_first, weight_second, targets):
@@ -585,30 +534,24 @@
         v((2, 2, 16, 16, 384), BF16),
         v((2, C1, C1), BF16),
         v((2, C1, C1), BF16),
-        v((8, 64, C0), F32),
         dma((4,)),
-        dma((16,)),
-        dma((16,)),
+        dma((3,)),
         dma((2, 2)),
         dma((2, 2)),
-        dma((2, 2, 16)),
-        dma((2, 2, 16)),
-        dma((2, 2, 8)),
-        dma((2, 2, 8)),
-        dma((2, 16)),
-        dma((2, 16)),
-        dma((2, 16)),
-        dma((2, 16)),
+        dma((2, 2, 2)),
+        dma((2, 2, 2)),
+        dma((2,)),
+        dma((2, 4)),
+        dma((2, 2)),
     ]
-    anywhere = pl.BlockSpec(memory_space=pl.ANY)
     return pl.pallas_call(
         kernel,
-        out_shape=jax.ShapeDtypeStruct((8, 64, C0), F32),
+        out_shape=pltpu.VMEM((8, 64, C0), F32),
         in_specs=[pl.BlockSpec(memory_space=pltpu.HBM)] * 4,
-        out_specs=anywhere,
+        out_specs=pl.BlockSpec(memory_space=pltpu.VMEM),
         scratch_shapes=scratch,
         compiler_params=pltpu.CompilerParams(
-            collective_id=0, has_side_effects=True, vmem_limit_bytes=56 * 1024 * 1024
+            collective_id=0, has_side_effects=True, vmem_limit_bytes=67043328 - 768 * 1024
         ),
         name="style_grad",
     )(

time: 57.9 us -> 52.4 us (0.905)
  Pallas kernels: 55.9 us -> 51.6 us
  local copies, waits for them, and re-layouts: 1.87 us -> 0.8 us
    pallas_call x1, Pallas kernels: 55.9 us -> 51.6 us  [local(): pl.pallas_call(kernel, out_shape=pltpu.VMEM((8, 64, C0), F32), in_specs=[...]
    unnamed x1, local copies, waits for them, and re-layouts: 1.87 us -> 0.8 us
where the time goes in v3:
time: 52.4 us
  Pallas kernels  51.6 us (98%)
  local copies, waits for them, and re-layouts  0.8 us (2%)
    pallas_call x1, Pallas kernels, local(): pl.pallas_call(kernel, out_shape=pltpu.VMEM((8, 64, C0), F32), in_specs=[...  51.6 us

profile of v3, /device:TPU:1, one launch (start us, length us, event | category | flops | bytes accessed | tf_op | source)
XLA Modules:
  0.0 52.4 jit_solution(15406630189478192568)
XLA Ops:
  0.0 51.6 %style_grad.1 = f32[8,64,256]{2,1,0:T(8,128)S(1)} custom-call(f32[8,64,256]{2,1,0:T(8,128)} %pool_hbm.1, bf16[3,768,512]{2,1,0:T(8,128)(2,1)} %bitcast.3, bf16[3,1536,512]{2,1,0:T(8,128)(2,1)} %bitcast.2, f32[2,512,512]{2,1,0:T(8,128)} %tg_hbm.1), custom_call_target="tpu_custom_call" | custom-call | tf_op jit(solution)/shard_map/style_grad/pallas_call | solution.py:547
  51.6 0.8 %copy.6 = f32[8,64,256]{2,1,0:T(8,128)} copy(f32[8,64,256]{2,1,0:T(8,128)S(1)} %style_grad.1) | data formatting | bytes 1048576

commit v4 on v3

--- a/solution.py
+++ b/solution.py
@@ -81,7 +81,6 @@
     )
     xy_others = [lax.rem(x + i, 4) * 4 + lax.rem(y + j, 4) for i, j in xy_steps]
     xy_from = [lax.rem(x + 4 - i, 4) * 4 + lax.rem(y + 4 - j, 4) for i, j in xy_steps]
-    ag_order = range(15)
     z_others = [lax.rem(z + i, 8) for i in (4, 3, 5, 2, 6, 1, 7)]
     sides = [(i, j) for i in (-1, 1) for j in (-1, 1, 0)] + [(0, -1), (0, 1)]
 
@@ -91,7 +90,7 @@
     loads = [
         pltpu.make_async_copy(source, target, local_sem.at[i])
         for i, (source, target) in enumerate(
-            ((pool_hbm, pool), (tg_hbm, tg), (w1_hbm, w1), (w2_hbm, w2))
+            ((pool_hbm, pool), (w1_hbm, w1), (tg_hbm, tg), (w2_hbm, w2))
         )
     ]
     for load in loads:
@@ -136,12 +135,36 @@
     def wait_all(part, sem):
         pltpu.make_async_copy(part, part, sem).wait()
 
+    def conv1_from(pieces):
+        total = None
+        for a in range(3):
+            left = [flat(xs[pl.ds(row + a, rows), col : col + cols]) for row, rows, col, cols in pieces]
+            part = dot_nn(jnp.concatenate(left, axis=0) if len(left) > 1 else left[0], w1[a])
+            total = part if total is None else total + part
+        at = 0
+        for row, rows, col, cols in pieces:
+            n = rows * cols
+            pre1[pl.ds(row, rows), col : col + cols] = total[at : at + n].reshape(rows, cols, C1)
+            at += n
+
+    def shift_inner(r, carry):
+        row = pool[r - 4].astype(BF16).astype(F32)
+        for b in range(3):
+            xs[r, 16:64, b * C0 : (b + 1) * C0] = ahead(row, b - 1)[8:56].astype(BF16)
+        return carry
+
+    def gelu_inner(r, carry):
+        act1[r, 16:64] = gelu_value(pre1[r, 16:64])
+        return carry
+
+    lax.fori_loop(4, 12, shift_inner, 0)
     loads[1].wait()
+    conv1_from([(4, 6, 16, 48)])
+    lax.fori_loop(4, 10, gelu_inner, 0)
+    loads[2].wait()
     for l in range(2):
         whole = tg[l]
         ts[l] = (whole + whole.T) * 0.5
-    loads[2].wait()
-    loads[3].wait()
     wait_all(pad.at[pl.ds(0, 7), pl.ds(0, 8)], halo_sem.at[1])
 
     def on_edges(top, bottom, left, right):
@@ -184,25 +207,20 @@
             xs[r, :, b * C0 : (b + 1) * C0] = ahead(row, b - 1).astype(BF16)
         return carry
 
-    def conv1(first, rows):
-        total = None
-        for a in range(3):
-            part = dot_nn(flat(xs[pl.ds(first + a, rows)]), w1[a])
-            total = part if total is None else total + part
-        pre1[pl.ds(first, rows)] = total.reshape(rows, W, C1)
-
     def gelu_row(r, carry):
         act1[r] = gelu_value(pre1[r])
         return carry
 
+    def gelu_sides(r, carry):
+        for col in (0, 64):
+            act1[r, col : col + 16] = gelu_value(pre1[r, col : col + 16])
+        return carry
+
     lax.fori_loop(2, 14, shift_pool, 0)
-
-    def conv1_step(i, carry):
-        conv1(2 + 5 * i, 5)
-        return carry
-
-    lax.fori_loop(0, 2, conv1_step, 0)
-    lax.fori_loop(2, 12, gelu_row, 0)
+    conv1_from([(2, 2, 0, W), (10, 2, 0, W), (4, 6, 0, 16), (4, 6, 64, 16)])
+    lax.fori_loop(2, 4, gelu_row, 0)
+    lax.fori_loop(4, 10, gelu_sides, 0)
+    lax.fori_loop(10, 12, gelu_row, 0)
     clear_edges(act1, 2, 10, 1)
 
     def shift_first(r, carry):
@@ -219,9 +237,17 @@
             device_id=who, device_id_type=MESH,
         )
 
-    def pair_piece(l):
+    def by_core(who, act):
+        pl.when(who == 0)(lambda: act(pl.ds(0, 384)))
+        pl.when(who == 1)(lambda: act(pl.ds(0, 256)))
+
+    def pair_piece(l, lanes):
         return remote(
-            s0.at[l, 1 - core], r0.at[l], pair_send.at[l, 0], pair_recv.at[l, 0], partner
+            s0.at[l, 1 - core, :, :, lanes],
+            r0.at[l, :, :, lanes],
+            pair_send.at[l, 0],
+            pair_recv.at[l, 0],
+            partner,
         )
 
     def pair_mean(l):
@@ -232,31 +258,31 @@
         other = means.at[l, 2 * k + 1 - core]
         return remote(other, other, pair_send.at[l, 1], pair_recv.at[l, 1], partner)
 
-    def rs_piece(l, other):
+    def rs_piece(l, other, lanes):
         return remote(
-            tsum.at[l, other], r1.at[l, k], rs_sem.at[l, 0, 0], rs_sem.at[l, 0, 1], xy_peer(other)
+            tsum.at[l, other, :, lanes], r1.at[l, k, :, lanes], rs_sem.at[l, 0, 0], rs_sem.at[l, 0, 1], xy_peer(other)
         )
 
     def rs_mean(l, other):
         both = means.at[l, pl.ds(2 * k, 2)]
         return remote(both, both, rs_sem.at[l, 1, 0], rs_sem.at[l, 1, 1], xy_peer(other))
 
-    def z_piece(l, other):
-        part = zb.at[l, z]
+    def z_piece(l, other, lanes):
+        part = zb.at[l, z, :, lanes]
         return remote(part, part, z_sem.at[l, 0, 0], z_sem.at[l, 0, 1], z_peer(other))
 
     def z_mean(l, other):
         part = zm.at[l, z]
         return remote(part, part, z_sem.at[l, 1, 0], z_sem.at[l, 1, 1], z_peer(other))
 
-    def ag_piece(l, n):
-        part = ga.at[l, core, k]
+    def ag_piece(l, n, lanes):
+        part = ga.at[l, core, k, :, lanes]
         return remote(
             part, part, ag_send.at[l], ag_recv.at[l, n // 4], xy_peer(xy_others[n])
         )
 
-    def fw_piece(l, slot):
-        part = ga.at[l, core, slot]
+    def fw_piece(l, slot, lanes):
+        part = ga.at[l, core, slot, :, lanes]
         return remote(part, part, fw_sem.at[l, 0], fw_sem.at[l, 1], partner)
 
     def local_gram(l, values):
@@ -266,23 +292,27 @@
         pair_mean(l).start()
         gram = lax.dot_general(cen, cen, (((0,), (0,)), ((), ())), preferred_element_type=F32)
         for i in range(4):
-            for d in range(3):
+            for d in range(3 if i < 2 else 2):
                 j = (i + d) % 4
                 block = gram[128 * i : 128 * i + 128, 128 * j : 128 * j + 128].astype(BF16)
                 s0[l, i // 2, (i % 2) * 8 : (i % 2) * 8 + 8, :, 128 * d : 128 * d + 128] = (
                     block.reshape(8, 16, 128)
                 )
-        pair_piece(l).start()
+        by_core(1 - core, lambda lanes: pair_piece(l, lanes).start())
 
     def rs_start(l):
         pair_mean_in(l).wait_recv()
         for other in xy_others:
             rs_mean(l, other).start()
-        pair_piece(l).wait_recv()
+        by_core(core, lambda lanes: wait_all(r0.at[l, :, :, lanes], pair_recv.at[l, 0]))
         tsum[l] = (s0[l, core].astype(F32) + r0[l].astype(F32)).astype(BF16)
         r1[l, k] = tsum[l, k]
-        for other in xy_others:
-            rs_piece(l, other).start()
+
+        def send(lanes):
+            for other in xy_others:
+                rs_piece(l, other, lanes).start()
+
+        by_core(core, send)
 
     def spread(rows):
         n = rows.shape[0]
@@ -303,33 +333,51 @@
         wait_all(means.at[l, pl.ds(0, 30)], rs_sem.at[l, 1, 1])
         mean, extra = spread(means[l].reshape(32, C1))
         zm[l, z] = mean
-        wait_all(r1.at[l, pl.ds(0, 15)], rs_sem.at[l, 0, 1])
+        by_core(
+            core,
+            lambda lanes: wait_all(r1.at[l, pl.ds(0, 15), :, lanes], rs_sem.at[l, 0, 1]),
+        )
+        for other in z_others:
+            z_mean(l, other).start()
         total = jnp.sum(r1[l].astype(F32), axis=0) + float(OWN) * extra
         zb[l, z] = total.astype(Z_TYPE)
-        for other in z_others:
-            z_mean(l, other).start()
-        for other in z_others:
-            z_piece(l, other).start()
+
+        def send(lanes):
+            for other in z_others:
+                z_piece(l, other, lanes).start()
+
+        by_core(core, send)
 
     def z_done(l):
         wait_all(zm.at[l, pl.ds(0, 7)], z_sem.at[l, 1, 1])
         mean, extra = spread(zm[l].reshape(8, C1))
-        wait_all(zb.at[l, pl.ds(0, 7)], z_sem.at[l, 0, 1])
+        by_core(
+            core, lambda lanes: wait_all(zb.at[l, pl.ds(0, 7), :, lanes], z_sem.at[l, 0, 1])
+        )
         total = jnp.sum(zb[l].astype(F32), axis=0) + float(32 * OWN) * extra
         ga[l, core, k] = (total * (1.0 / CELLS)).astype(BF16)
-        for n in ag_order:
-            ag_piece(l, n).start()
-        fw_piece(l, k).start()
+
+        def send(lanes):
+            for n in range(15):
+                ag_piece(l, n, lanes).start()
+            fw_piece(l, k, lanes).start()
+
+        by_core(core, send)
         return mean
 
     def gathered(l):
-        for n in ag_order:
-            if n % 4 == 0:
-                wait_all(ga.at[l, core, pl.ds(0, min(4, 15 - n))], ag_recv.at[l, n // 4])
-            fw_piece(l, xy_from[n]).start()
+        def forward(lanes):
+            for n in range(15):
+                if n % 4 == 0:
+                    wait_all(
+                        ga.at[l, core, pl.ds(0, min(4, 15 - n)), :, lanes], ag_recv.at[l, n // 4]
+                    )
+                fw_piece(l, xy_from[n], lanes).start()
+
+        by_core(core, forward)
 
     def forwarded(l):
-        wait_all(ga.at[l, 1 - core], fw_sem.at[l, 1])
+        by_core(1 - core, lambda lanes: wait_all(ga.at[l, 1 - core, :, :, lanes], fw_sem.at[l, 1]))
 
     def mismatch(l):
         def put(i, j, block):
@@ -341,14 +389,16 @@
             ).astype(BF16)
 
         for i in range(4):
-            rows = ga[l, i // 2, (i % 2) * 8 : (i % 2) * 8 + 8].astype(F32).reshape(128, 384)
-            for d in range(3):
-                block = rows[:, 128 * d : 128 * d + 128]
+            for d in range(3 if i < 2 else 2):
+                block = ga[l, i // 2, (i % 2) * 8 : (i % 2) * 8 + 8, :, 128 * d : 128 * d + 128]
+                block = block.astype(F32).reshape(128, 128)
                 put(i, (i + d) % 4, block)
-                if d == 1:
-                    put((i + 1) % 4, i, block.T)
+                if d > 0:
+                    put((i + d) % 4, i, block.T)
 
     local_gram(0, flat(act1[3:11, 8:72, :]))
+
+    loads[3].wait()
 
     def conv2_main(i, carry):
         total = None
@@ -368,14 +418,8 @@
     lax.fori_loop(0, 2, shift_pool, 0)
     lax.fori_loop(14, 16, shift_pool, 0)
 
-    def conv1_rim(i, carry):
-        conv1(12 * i, 2)
-        return carry
-
-    lax.fori_loop(0, 2, conv1_rim, 0)
+    conv1_from([(0, 2, 0, W), (12, 2, 0, W)])
     rs_start(1)
-
-    plane_done(0)
 
     def finish_first(r, carry):
         value, slope = gelu_both(pre1[r])
@@ -383,35 +427,34 @@
         sl1[r] = slope
         return carry
 
-    lax.fori_loop(0, 14, finish_first, 0)
-    clear_edges(act1, 0, 14, 3)
-    clear_edges(sl1, 2, 10, 1)
-
     def shift_first_all(r, carry):
         row = act1[r]
         for b in range(3):
             fs[r, :, b * C1 : (b + 1) * C1] = ahead(row, b - 1).astype(BF16)
         return carry
 
-    lax.fori_loop(0, 14, shift_first_all, 0)
-
-    plane_done(1)
-
     def conv2_all(i, carry):
         total = None
         for a in range(3):
-            part = dot_nn(flat(fs[pl.ds(4 * i + a, 4)]), w2[a])
+            part = dot_nn(flat(fs[pl.ds(3 * i + a, 3)]), w2[a])
             total = part if total is None else total + part
         value, slope = gelu_both(total)
-        act2[pl.ds(4 * i, 4)] = value.reshape(4, W, C1)
-        sl2[pl.ds(4 * i, 4)] = slope.reshape(4, W, C1)
-        return carry
-
+        act2[pl.ds(3 * i, 3)] = value.reshape(3, W, C1)
+        sl2[pl.ds(3 * i, 3)] = slope.reshape(3, W, C1)
+        return carry
+
+    lax.fori_loop(0, 14, finish_first, 0)
+    clear_edges(act1, 0, 14, 3)
+    clear_edges(sl1, 2, 10, 1)
+    plane_done(0)
+    lax.fori_loop(0, 14, shift_first_all, 0)
     lax.fori_loop(0, 1, conv2_all, 0)
+    plane_done(1)
+    lax.fori_loop(1, 2, conv2_all, 0)
     mean_first = z_done(0)
-    lax.fori_loop(1, 2, conv2_all, 0)
+    lax.fori_loop(2, 3, conv2_all, 0)
     mean_second = z_done(1)
-    lax.fori_loop(2, 3, conv2_all, 0)
+    lax.fori_loop(3, 4, conv2_all, 0)
     clear_edges(sl2, 0, 12, 2)
 
     def centre(source, high, low, mean, shift):
@@ -439,11 +482,15 @@
     gathered(0)
     wait_all(pad.at[pl.ds(0, 12), pl.ds(0, 8)], halo_sem.at[0])
     for l in range(2):
-        pair_piece(l).wait_send()
+        by_core(1 - core, lambda lanes: wait_all(r0.at[l, :, :, lanes], pair_send.at[l, 0]))
         pair_mean(l).wait_send()
-        wait_all(r1.at[l, pl.ds(0, 15)], rs_sem.at[l, 0, 0])
+
+        def sent(lanes):
+            wait_all(r1.at[l, pl.ds(0, 15), :, lanes], rs_sem.at[l, 0, 0])
+            wait_all(zb.at[l, pl.ds(0, 7), :, lanes], z_sem.at[l, 0, 0])
+
+        by_core(core, sent)
         wait_all(means.at[l, pl.ds(0, 30)], rs_sem.at[l, 1, 0])
-        wait_all(zb.at[l, pl.ds(0, 7)], z_sem.at[l, 0, 0])
         wait_all(zm.at[l, pl.ds(0, 7)], z_sem.at[l, 1, 0])
     forwarded(0)
     mismatch(0)
@@ -482,8 +529,12 @@
     lax.fori_loop(0, 2, back1, 0)
 
     for l in range(2):
-        wait_all(ga.at[l, core, pl.ds(0, 15)], ag_send.at[l])
-        wait_all(ga.at[l, core], fw_sem.at[l, 0])
+
+        def gone(lanes):
+            wait_all(ga.at[l, core, pl.ds(0, 15), :, lanes], ag_send.at[l])
+            wait_all(ga.at[l, core, :, :, lanes], fw_sem.at[l, 0])
+
+        by_core(core, gone)
 
     def back0(i, carry):
         total = None

time: 52.4 us -> 50.6 us (0.966)
  Pallas kernels: 51.6 us -> 49.7 us
    pallas_call x1, Pallas kernels: 51.6 us -> 49.7 us  [local(): pl.pallas_call(kernel, out_shape=pltpu.VMEM((8, 64, C0), F32), in_specs=[...]
where the time goes in v4:
time: 50.6 us; the launch traced here: 50.5 us
  Pallas kernels  49.7 us (98%)
  local copies, waits for them, and re-layouts  0.8 us (2%)
    pallas_call x1, Pallas kernels, local(): pl.pallas_call(kernel, out_shape=pltpu.VMEM((8, 64, C0), F32), in_specs=[...  49.7 us

profile of v4, /device:TPU:1, one launch (start us, length us, event | category | flops | bytes accessed | tf_op | source)
XLA Modules:
  0.0 50.5 jit_solution(17800347431064782560)
XLA Ops:
  0.0 49.7 %style_grad.1 = f32[8,64,256]{2,1,0:T(8,128)S(1)} custom-call(f32[8,64,256]{2,1,0:T(8,128)} %pool_hbm.1, bf16[3,768,512]{2,1,0:T(8,128)(2,1)} %bitcast.3, bf16[3,1536,512]{2,1,0:T(8,128)(2,1)} %bitcast.2, f32[2,512,512]{2,1,0:T(8,128)} %tg_hbm.1), custom_call_target="tpu_custom_call" | custom-call | tf_op jit(solution)/shard_map/style_grad/pallas_call | solution.py:598
  49.7 0.8 %copy.6 = f32[8,64,256]{2,1,0:T(8,128)} copy(f32[8,64,256]{2,1,0:T(8,128)S(1)} %style_grad.1) | data formatting | bytes 1048576

commit v5 on v4

--- a/solution.py
+++ b/solution.py
@@ -93,7 +93,7 @@
             ((pool_hbm, pool), (w1_hbm, w1), (tg_hbm, tg), (w2_hbm, w2))
         )
     ]
-    for load in loads:
+    for load in loads[:2]:
         load.start()
     barrier = pltpu.get_barrier_semaphore()
 
@@ -109,31 +109,14 @@
     greet(partner)
     loads[0].wait()
     pad[4:12, 1:9] = pool[...].astype(BF16).reshape(8, 8, 8, C0)
-    pl.semaphore_wait(barrier, 31)
-
-    cols_from = {1: (8, 1), 0: (1, 8), -1: (1, 1)}
-    cols_to = {1: (0, 1), 0: (1, 8), -1: (9, 1)}
-
-    def halo(i, j, row_from, row_to, rows, arrival):
-        (fc, nc), (tc, _) = cols_from[j], cols_to[j]
-        return pltpu.make_async_remote_copy(
-            src_ref=pad.at[pl.ds(row_from, rows), pl.ds(fc, nc)],
-            dst_ref=pad.at[pl.ds(row_to, rows), pl.ds(tc, nc)],
-            send_sem=halo_sem.at[0],
-            recv_sem=halo_sem.at[arrival],
-            device_id=side_peer(i, j),
-            device_id_type=MESH,
-        )
-
-    near_rows = {1: (10, 2, 2), 0: (4, 4, 8), -1: (4, 12, 2)}
-    far_rows = {1: (8, 0, 2), -1: (6, 14, 2)}
-    near = [halo(i, j, *near_rows[i], 1) for i, j in sides]
-    far = [halo(i, j, *far_rows[i], 2) for i, j in sides if i != 0]
-    for copy in near + far:
-        copy.start()
-
-    def wait_all(part, sem):
-        pltpu.make_async_copy(part, part, sem).wait()
+    def rows_loop(first, last, step, at_once):
+        def some(i, carry):
+            for n in range(at_once):
+                step(first + i * at_once + n, carry)
+            return carry
+
+        times = (last - first) // at_once
+        lax.fori_loop(0, times, some, 0, unroll=times == 1)
 
     def conv1_from(pieces):
         total = None
@@ -157,10 +140,38 @@
         act1[r, 16:64] = gelu_value(pre1[r, 16:64])
         return carry
 
-    lax.fori_loop(4, 12, shift_inner, 0)
+    rows_loop(4, 12, shift_inner, 4)
     loads[1].wait()
+    for load in loads[2:]:
+        load.start()
     conv1_from([(4, 6, 16, 48)])
-    lax.fori_loop(4, 10, gelu_inner, 0)
+    rows_loop(4, 10, gelu_inner, 3)
+    pl.semaphore_wait(barrier, 31)
+
+    cols_from = {1: (8, 1), 0: (1, 8), -1: (1, 1)}
+    cols_to = {1: (0, 1), 0: (1, 8), -1: (9, 1)}
+
+    def halo(i, j, row_from, row_to, rows, arrival):
+        (fc, nc), (tc, _) = cols_from[j], cols_to[j]
+        return pltpu.make_async_remote_copy(
+            src_ref=pad.at[pl.ds(row_from, rows), pl.ds(fc, nc)],
+            dst_ref=pad.at[pl.ds(row_to, rows), pl.ds(tc, nc)],
+            send_sem=halo_sem.at[0],
+            recv_sem=halo_sem.at[arrival],
+            device_id=side_peer(i, j),
+            device_id_type=MESH,
+        )
+
+    near_rows = {1: (10, 2, 2), 0: (4, 4, 8), -1: (4, 12, 2)}
+    far_rows = {1: (8, 0, 2), -1: (6, 14, 2)}
+    near = [halo(i, j, *near_rows[i], 1) for i, j in sides]
+    far = [halo(i, j, *far_rows[i], 2) for i, j in sides if i != 0]
+    for copy in near + far:
+        copy.start()
+
+    def wait_all(part, sem):
+        pltpu.make_async_copy(part, part, sem).wait()
+
     loads[2].wait()
     for l in range(2):
         whole = tg[l]
@@ -216,11 +227,12 @@
             act1[r, col : col + 16] = gelu_value(pre1[r, col : col + 16])
         return carry
 
-    lax.fori_loop(2, 14, shift_pool, 0)
-    conv1_from([(2, 2, 0, W), (10, 2, 0, W), (4, 6, 0, 16), (4, 6, 64, 16)])
-    lax.fori_loop(2, 4, gelu_row, 0)
-    lax.fori_loop(4, 10, gelu_sides, 0)
-    lax.fori_loop(10, 12, gelu_row, 0)
+    rows_loop(2, 14, shift_pool, 4)
+    conv1_from([(2, 2, 0, W), (10, 2, 0, W)])
+    rows_loop(2, 4, gelu_row, 2)
+    rows_loop(10, 12, gelu_row, 2)
+    conv1_from([(4, 6, 0, 16), (4, 6, 64, 16)])
+    rows_loop(4, 10, gelu_sides, 6)
     clear_edges(act1, 2, 10, 1)
 
     def shift_first(r, carry):
@@ -229,7 +241,7 @@
             fsm[r, :, b * C1 : (b + 1) * C1] = ahead(row, b - 1)[8:72].astype(BF16)
         return carry
 
-    lax.fori_loop(0, 10, shift_first, 0)
+    rows_loop(0, 10, shift_first, 5)
 
     def remote(source, target, send, recv, who):
         return pltpu.make_async_remote_copy(
@@ -408,15 +420,15 @@
         act2m[pl.ds(4 * i, 4)] = gelu_value(total).reshape(4, 64, C1)
         return carry
 
-    lax.fori_loop(0, 1, conv2_main, 0)
+    conv2_main(0, 0)
     rs_start(0)
-    lax.fori_loop(1, 2, conv2_main, 0)
+    conv2_main(1, 0)
     local_gram(1, flat(act2m[...]))
 
     wait_all(pad.at[pl.ds(0, 5), pl.ds(0, 8)], halo_sem.at[2])
     clear_pad(0, 14, ((0, 2), (14, 2)))
-    lax.fori_loop(0, 2, shift_pool, 0)
-    lax.fori_loop(14, 16, shift_pool, 0)
+    rows_loop(0, 2, shift_pool, 2)
+    rows_loop(14, 16, shift_pool, 2)
 
     conv1_from([(0, 2, 0, W), (12, 2, 0, W)])
     rs_start(1)
@@ -443,18 +455,18 @@
         sl2[pl.ds(3 * i, 3)] = slope.reshape(3, W, C1)
         return carry
 
-    lax.fori_loop(0, 14, finish_first, 0)
+    rows_loop(0, 14, finish_first, 2)
     clear_edges(act1, 0, 14, 3)
     clear_edges(sl1, 2, 10, 1)
     plane_done(0)
-    lax.fori_loop(0, 14, shift_first_all, 0)
-    lax.fori_loop(0, 1, conv2_all, 0)
+    rows_loop(0, 14, shift_first_all, 7)
+    conv2_all(0, 0)
     plane_done(1)
-    lax.fori_loop(1, 2, conv2_all, 0)
+    conv2_all(1, 0)
     mean_first = z_done(0)
-    lax.fori_loop(2, 3, conv2_all, 0)
+    conv2_all(2, 0)
     mean_second = z_done(1)
-    lax.fori_loop(3, 4, conv2_all, 0)
+    conv2_all(3, 0)
     clear_edges(sl2, 0, 12, 2)
 
     def centre(source, high, low, mean, shift):
@@ -467,8 +479,8 @@
 
         return step
 
-    lax.fori_loop(0, 10, centre(act1, ch1, cl1, mean_first, 2), 0)
-    lax.fori_loop(0, 12, centre(act2, ch2, cl2, mean_second, 0), 0)
+    rows_loop(0, 10, centre(act1, ch1, cl1, mean_first, 2), 5)
+    rows_loop(0, 12, centre(act2, ch2, cl2, mean_second, 0), 4)
 
     def push(l, high, low, first, rows):
         top = flat(high[pl.ds(first, rows)])
@@ -494,9 +506,9 @@
         wait_all(zm.at[l, pl.ds(0, 7)], z_sem.at[l, 1, 0])
     forwarded(0)
     mismatch(0)
-    lax.fori_loop(0, 1, push_first, 0)
+    push_first(0, 0)
     gathered(1)
-    lax.fori_loop(1, 2, push_first, 0)
+    push_first(1, 0)
     forwarded(1)
 
     mismatch(1)
@@ -509,7 +521,7 @@
             )
         return carry
 
-    lax.fori_loop(0, 3, back2, 0)
+    lax.fori_loop(0, 3, back2, 0, unroll=True)
 
     def back1(i, carry):
         flow = flat(flow1[pl.ds(5 * i, 5)])
@@ -526,7 +538,7 @@
             )
         return carry
 
-    lax.fori_loop(0, 2, back1, 0)
+    lax.fori_loop(0, 2, back1, 0, unroll=True)
 
     for l in range(2):
 
@@ -548,7 +560,7 @@
         out[pl.ds(4 * i, 4)] = total.reshape(4, 64, C0)
         return carry
 
-    lax.fori_loop(0, 2, back0, 0)
+    lax.fori_loop(0, 2, back0, 0, unroll=True)
 
 
 def local(pool_input, weight_first, weight_second, targets):

time: 50.6 us -> 49.2 us (0.972)
  Pallas kernels: 49.7 us -> 48.3 us
    pallas_call x1, Pallas kernels: 49.7 us -> 48.3 us  [local(): pl.pallas_call(kernel, out_shape=pltpu.VMEM((8, 64, C0), F32), in_specs=[...]
where the time goes in v5:
time: 49.2 us; the launch traced here: 49.1 us
  Pallas kernels  48.3 us (98%)
  local copies, waits for them, and re-layouts  0.8 us (2%)
    pallas_call x1, Pallas kernels, local(): pl.pallas_call(kernel, out_shape=pltpu.VMEM((8, 64, C0), F32), in_specs=[...  48.3 us

profile of v5, /device:TPU:1, one launch (start us, length us, event | category | flops | bytes accessed | tf_op | source)
XLA Modules:
  0.0 49.1 jit_solution(6875721360415339540)
XLA Ops:
  0.0 48.3 %style_grad.1 = f32[8,64,256]{2,1,0:T(8,128)S(1)} custom-call(f32[8,64,256]{2,1,0:T(8,128)} %pool_hbm.1, bf16[3,768,512]{2,1,0:T(8,128)(2,1)} %bitcast.3, bf16[3,1536,512]{2,1,0:T(8,128)(2,1)} %bitcast.2, f32[2,512,512]{2,1,0:T(8,128)} %tg_hbm.1), custom_call_target="tpu_custom_call" | custom-call | tf_op jit(solution)/shard_map/style_grad/pallas_call | solution.py:610
  48.3 0.8 %copy.6 = f32[8,64,256]{2,1,0:T(8,128)} copy(f32[8,64,256]{2,1,0:T(8,128)S(1)} %style_grad.1) | data formatting | bytes 1048576

commit v6 on v5

--- a/solution.py
+++ b/solution.py
@@ -90,10 +90,17 @@
     loads = [
         pltpu.make_async_copy(source, target, local_sem.at[i])
         for i, (source, target) in enumerate(
-            ((pool_hbm, pool), (w1_hbm, w1), (tg_hbm, tg), (w2_hbm, w2))
+            (
+                (pool_hbm, pool),
+                (w1_hbm.at[0], w1.at[0]),
+                (w1_hbm.at[1], w1.at[1]),
+                (w1_hbm.at[2], w1.at[2]),
+                (tg_hbm, tg),
+                (w2_hbm, w2),
+            )
         )
     ]
-    for load in loads[:2]:
+    for load in loads[:4]:
         load.start()
     barrier = pltpu.get_barrier_semaphore()
 
@@ -118,9 +125,11 @@
         times = (last - first) // at_once
         lax.fori_loop(0, times, some, 0, unroll=times == 1)
 
-    def conv1_from(pieces):
+    def conv1_from(pieces, weights=None):
         total = None
         for a in range(3):
+            if weights is not None:
+                weights[a].wait()
             left = [flat(xs[pl.ds(row + a, rows), col : col + cols]) for row, rows, col, cols in pieces]
             part = dot_nn(jnp.concatenate(left, axis=0) if len(left) > 1 else left[0], w1[a])
             total = part if total is None else total + part
@@ -141,10 +150,9 @@
         return carry
 
     rows_loop(4, 12, shift_inner, 4)
-    loads[1].wait()
-    for load in loads[2:]:
+    conv1_from([(4, 6, 16, 48)], loads[1:4])
+    for load in loads[4:]:
         load.start()
-    conv1_from([(4, 6, 16, 48)])
     rows_loop(4, 10, gelu_inner, 3)
     pl.semaphore_wait(barrier, 31)
 
@@ -166,17 +174,19 @@
     far_rows = {1: (8, 0, 2), -1: (6, 14, 2)}
     near = [halo(i, j, *near_rows[i], 1) for i, j in sides]
     far = [halo(i, j, *far_rows[i], 2) for i, j in sides if i != 0]
-    for copy in near + far:
+    for copy in near:
         copy.start()
 
     def wait_all(part, sem):
         pltpu.make_async_copy(part, part, sem).wait()
 
-    loads[2].wait()
+    loads[4].wait()
     for l in range(2):
         whole = tg[l]
         ts[l] = (whole + whole.T) * 0.5
     wait_all(pad.at[pl.ds(0, 7), pl.ds(0, 8)], halo_sem.at[1])
+    for copy in far:
+        copy.start()
 
     def on_edges(top, bottom, left, right):
         pl.when(g == 0)(top)
@@ -410,7 +420,7 @@
 
     local_gram(0, flat(act1[3:11, 8:72, :]))
 
-    loads[3].wait()
+    loads[5].wait()
 
     def conv2_main(i, carry):
         total = None
@@ -597,7 +607,7 @@
         v((2, 2, 16, 16, 384), BF16),
         v((2, C1, C1), BF16),
         v((2, C1, C1), BF16),
-        dma((4,)),
+        dma((6,)),
         dma((3,)),
         dma((2, 2)),
         dma((2, 2)),

time: 49.2 us -> 48.6 us (0.988)
  Pallas kernels: 48.3 us -> 47.7 us
    pallas_call x1, Pallas kernels: 48.3 us -> 47.7 us  [local(): pl.pallas_call(kernel, out_shape=pltpu.VMEM((8, 64, C0), F32), in_specs=[...]
where the time goes in v6:
time: 48.6 us; the launch traced here: 48.5 us
  Pallas kernels  47.7 us (98%)
  local copies, waits for them, and re-layouts  0.8 us (2%)
    pallas_call x1, Pallas kernels, local(): pl.pallas_call(kernel, out_shape=pltpu.VMEM((8, 64, C0), F32), in_specs=[...  47.7 us

profile of v6, /device:TPU:1, one launch (start us, length us, event | category | flops | bytes accessed | tf_op | source)
XLA Modules:
  0.0 48.5 jit_solution(9957854157949502875)
XLA Ops:
  0.0 47.7 %style_grad.1 = f32[8,64,256]{2,1,0:T(8,128)S(1)} custom-call(f32[8,64,256]{2,1,0:T(8,128)} %pool_hbm.1, bf16[3,768,512]{2,1,0:T(8,128)(2,1)} %bitcast.3, bf16[3,1536,512]{2,1,0:T(8,128)(2,1)} %bitcast.2, f32[2,512,512]{2,1,0:T(8,128)} %tg_hbm.1), custom_call_target="tpu_custom_call" | custom-call | tf_op jit(solution)/shard_map/style_grad/pallas_call | solution.py:620
  47.7 0.8 %copy.6 = f32[8,64,256]{2,1,0:T(8,128)} copy(f32[8,64,256]{2,1,0:T(8,128)S(1)} %style_grad.1) | data formatting | bytes 1048576

commit v7 on v6

--- a/solution.py
+++ b/solution.py
@@ -322,10 +322,12 @@
                 )
         by_core(1 - core, lambda lanes: pair_piece(l, lanes).start())
 
-    def rs_start(l):
+    def rs_means(l):
         pair_mean_in(l).wait_recv()
         for other in xy_others:
             rs_mean(l, other).start()
+
+    def rs_start(l):
         by_core(core, lambda lanes: wait_all(r0.at[l, :, :, lanes], pair_recv.at[l, 0]))
         tsum[l] = (s0[l, core].astype(F32) + r0[l].astype(F32)).astype(BF16)
         r1[l, k] = tsum[l, k]
@@ -431,6 +433,7 @@
         return carry
 
     conv2_main(0, 0)
+    rs_means(0)
     rs_start(0)
     conv2_main(1, 0)
     local_gram(1, flat(act2m[...]))
@@ -440,6 +443,7 @@
     rows_loop(0, 2, shift_pool, 2)
     rows_loop(14, 16, shift_pool, 2)
 
+    rs_means(1)
     conv1_from([(0, 2, 0, W), (12, 2, 0, W)])
     rs_start(1)
 

time: 48.6 us -> 48.4 us (level)
  no operation moved by 1% of the time
where the time goes in v7:
time: 48.4 us; the launch traced here: 48.3 us
  Pallas kernels  47.5 us (98%)
  local copies, waits for them, and re-layouts  0.8 us (2%)
    pallas_call x1, Pallas kernels, local(): pl.pallas_call(kernel, out_shape=pltpu.VMEM((8, 64, C0), F32), in_specs=[...  47.5 us

profile of v7, /device:TPU:1, one launch (start us, length us, event | category | flops | bytes accessed | tf_op | source)
XLA Modules:
  0.0 48.3 jit_solution(13937017539428424914)
XLA Ops:
  0.0 47.5 %style_grad.1 = f32[8,64,256]{2,1,0:T(8,128)S(1)} custom-call(f32[8,64,256]{2,1,0:T(8,128)} %pool_hbm.1, bf16[3,768,512]{2,1,0:T(8,128)(2,1)} %bitcast.3, bf16[3,1536,512]{2,1,0:T(8,128)(2,1)} %bitcast.2, f32[2,512,512]{2,1,0:T(8,128)} %tg_hbm.1), custom_call_target="tpu_custom_call" | custom-call | tf_op jit(solution)/shard_map/style_grad/pallas_call | solution.py:624
  47.5 0.8 %copy.6 = f32[8,64,256]{2,1,0:T(8,128)} copy(f32[8,64,256]{2,1,0:T(8,128)S(1)} %style_grad.1) | data formatting | bytes 1048576
